TPU v7x, 128 devices: a whole 4x4x4 slice. The times are simulated.
128 devices in a mesh: grp: 2 (over x_lo), gr: 8 (over z, x_hi), gc: 8 (over y, core).
Axes of the slice: x: 4 (x_hi: 2, x_lo: 2; x = x_hi * 2 + x_lo), y: 4, z: 4, core: 2. Of those that a mesh axis runs over, the one named last changes fastest.
Arguments:
- embeddings: bfloat16 [131072, 768], P(('grp', 'gr', 'gc')), parts along dimension 0, may hold values from -2000 to 2000
- sorted_slot: int32 [131072], P(('grp', 'gr', 'gc')), parts along dimension 0, may hold values from 0 to 65535, as said below
- cluster_ids: int32 [131072], P(('grp', 'gr', 'gc')), parts along dimension 0, may hold values from 0 to 31, never falling along the last dimension, each value on 1 to 5120 neighbouring positions
- block_list: int32 [128, 4], P(('grp', 'gr', 'gc')), parts along dimension 0, may hold values 0 or 1
Outputs:
- dedup_weight: float32 [131072], P(('grp', 'gr', 'gc')), parts along dimension 0
There are 2 independent parts, one for each index of `grp`. A program takes and returns all parts, laid end to end along the dimension named above; each array names one. Nothing has to cross between parts.
Inputs may be any that keep to these rules, and one draw needn't show every extreme that they name: `sorted_slot`: a permutation; the 1024 encoder-order rows of each block hold exactly 16 positions in each block of cluster-sorted rows. `cluster_ids`: ids never fall along the cluster-sorted rows.
All inputs are finite; a program needn't handle non-finite values. No bound on the sum of `block_list` on one device may be relied on, other than what follows from the above.
Results may differ from a plain program's by a relative error of at most 0.00044.
Values may be sent and summed in bfloat16 or wider, within the bound.
No kernel may reach another device: no remote copies, remote signals or barrier semaphores. Data moves between devices by JAX's collectives and lax.ppermute only.
A program may use at most 64 MiB of HBM per device.

v0:
```python
import functools
import math

import jax
import jax.numpy as jnp
from jax import lax
from jax.experimental import pallas as pl
from jax.experimental.pallas import tpu as pltpu
from jax.sharding import PartitionSpec as P

SHIFTS = 4
ROWS = 1024
WIDTH = 768
LANES = 128
HINT = 20
COPIES = 3
APART = 2
PER_PAIR = 16
PIECES = WIDTH // LANES
MESSAGE = (COPIES * PIECES + 1) * PER_PAIR
TAIL = 16
DIGITS = 32
AXES = ("gr", "gc")

sharpness = 20.0
threshold = 0.8

F32 = jnp.float32
BF16 = jnp.bfloat16
VMEM = pl.BlockSpec(memory_space=pltpu.VMEM)
ANY = pl.BlockSpec(memory_space=pl.ANY)
SMEM = pl.BlockSpec(memory_space=pltpu.SMEM)


def iota(shape, axis):
    return lax.broadcasted_iota(jnp.int32, shape, axis)


def one_hot(rows, first, wanted):
    hit = iota((rows, wanted.shape[1]), 0) + first == wanted
    return jnp.where(hit, 1.0, 0.0).astype(BF16)


def nt(a, b):
    return lax.dot_general(a, b, (((1,), (1,)), ((), ())), preferred_element_type=F32)


def as_column(row):
    return jnp.transpose(jnp.broadcast_to(row, (LANES, row.shape[1])))


def front_kernel(devices, slot_hbm, emb_ref, out_hbm, slot_ref, raw_ref, unit_ref, digit_ref, out_ref, sems):
    size = 256
    parts = [pl.ds(at, size) for at in range(0, ROWS, size)]
    slots = pltpu.make_async_copy(slot_hbm, slot_ref, sems.at[len(parts)])
    slots.start()
    copies = []
    for n, part in enumerate(parts):
        copies.append(pltpu.make_async_copy(emb_ref.at[part, :], raw_ref.at[part, :], sems.at[n]))
        copies[n].start()
    before = jnp.where(iota((size, size), 0) < iota((size, size), 1), 1.0, 0.0).astype(BF16)
    slots.wait()
    slot = slot_ref[...]
    target = slot // ROWS
    low = slot - target * ROWS
    goes = iota((devices, ROWS), 0) == target
    goes_b = jnp.where(goes, 1.0, 0.0).astype(BF16)
    seen, ranks = jnp.zeros((devices, 1), F32), []
    for at in range(0, ROWS, size):
        here = goes[:, at:at + size]
        count = jnp.dot(goes_b[:, at:at + size], before, preferred_element_type=F32) + seen
        ranks.append(jnp.sum(jnp.where(here, count, 0.0), axis=0, keepdims=True))
        seen = seen + jnp.sum(jnp.where(here, 1.0, 0.0), axis=1, keepdims=True)
    rank = jnp.concatenate(ranks, axis=1)
    dest = target * PER_PAIR + rank.astype(jnp.int32)
    high = low // DIGITS
    even = iota((ROWS, LANES), 1) % 2 == 0
    digits = jnp.where(even, as_column(high.astype(F32)), as_column((low - high * DIGITS).astype(F32)))
    unit_ref[:, WIDTH:] = digits.astype(BF16)
    for n, part in enumerate(parts):
        copies[n].wait()
        values = raw_ref[part, :].astype(F32)
        mean = jnp.sum(values * values, axis=1, keepdims=True) * (1.0 / WIDTH)
        inverse = lax.rsqrt(mean + 1e-06) * (1.0 / math.sqrt(WIDTH))
        unit_ref[part, 0:WIDTH] = (values * inverse).astype(BF16)
    reach = APART * (COPIES - 1)
    per_part = size // PER_PAIR
    back = []

    def send(first, count):
        for device in range(first, first + count):
            tile = digit_ref[device * PER_PAIR:(device + 1) * PER_PAIR, :]
            for copy in range(1, COPIES):
                at = (device + APART * copy) % devices * PER_PAIR
                tile = jnp.where(lane == copy, digit_ref[at:at + PER_PAIR, :], tile)
            out_ref[(device + 1) * MESSAGE - PER_PAIR:(device + 1) * MESSAGE, :] = tile
        rows = pl.ds(first * MESSAGE, count * MESSAGE)
        back.append(pltpu.make_async_copy(out_ref.at[rows, :], out_hbm.at[rows, :], sems.at[len(back)]))
        back[-1].start()

    lane = iota((PER_PAIR, LANES), 1) // 2
    for n, part in enumerate(parts):
        place = one_hot(size, n * size, dest)
        placed = jnp.dot(place, unit_ref[...], preferred_element_type=F32).astype(BF16)
        digit_ref[part, :] = placed[:, WIDTH:]
        for i in range(per_part):
            block = n * per_part + i
            rows = placed[i * PER_PAIR:(i + 1) * PER_PAIR, :]
            for copy in range(COPIES):
                at = (block - APART * copy) % devices * MESSAGE + copy * PIECES * PER_PAIR
                for piece in range(PIECES):
                    out_ref[at + piece * PER_PAIR:at + (piece + 1) * PER_PAIR, :] = rows[:, piece * LANES:(piece + 1) * LANES]
        if n == 0:
            send(0, per_part - reach)
        else:
            send(n * per_part - reach, per_part)
    send(devices - reach, reach)
    for copy in back:
        copy.wait()


def tiles(got_hbm, copy, target, sem):
    started = []
    for piece in range(PIECES):
        at = (copy * PIECES + piece) * PER_PAIR
        lanes = pl.ds(piece * LANES, LANES)
        started.append(pltpu.make_async_copy(got_hbm.at[:, pl.ds(at, PER_PAIR), :], target.at[:, :, lanes], sem.at[piece]))
        started[-1].start()
    return started


def slot_tiles(got_hbm, target, sem):
    copy = pltpu.make_async_copy(got_hbm.at[:, pl.ds(MESSAGE - PER_PAIR, PER_PAIR), :], target, sem)
    copy.start()
    return copy


def arrival_slots(digits, copies):
    digits = jnp.transpose(digits.reshape(ROWS, LANES).astype(F32))[0:8, :]
    return [(digits[2 * c:2 * c + 1, :] * DIGITS + digits[2 * c + 1:2 * c + 2, :]).astype(jnp.int32) for c in copies]


def arrival_ids(ids, land):
    ids = jnp.broadcast_to(ids.astype(F32), (8, ROWS)).astype(BF16)
    arrived = jnp.zeros((8, ROWS), F32)
    for at in range(0, ROWS, 256):
        place = one_hot(256, at, land)
        arrived = arrived + jnp.dot(ids[:, at:at + 256], place, preferred_element_type=F32)
    return arrived[0:1, :]


def split_kernel(got_hbm, list_ref, *refs):
    ids_refs, (out_ref, blocks_ref, far_ref, land_ref, digit_ref, sems) = refs[:COPIES], refs[COPIES:]
    slots = slot_tiles(got_hbm, digit_ref, sems.at[0, PIECES])
    rows = [tiles(got_hbm, c, blocks_ref.at[c], sems.at[c]) for c in range(COPIES)]
    slots.wait()
    lands = arrival_slots(digit_ref[...], range(COPIES))
    land_ref[...] = lands[0]
    for c in range(COPIES):
        far_ref[c] = arrival_ids(ids_refs[c][...], lands[c])
    ids = far_ref[0]
    entries = list_ref[...].astype(F32)
    row = iota((TAIL, LANES), 0)
    for at in range(0, WIDTH, LANES):
        rest = ids[:, at + WIDTH:at + WIDTH + LANES] if at + WIDTH < ROWS else jnp.zeros((1, LANES), F32)
        tail = jnp.where(row == 0, ids[:, at:at + LANES], jnp.where(row == 1, rest, entries))
        out_ref[ROWS:ROWS + TAIL, at:at + LANES] = tail.astype(BF16)
    for copy in rows[0]:
        copy.wait()
    out_ref[0:ROWS, :] = blocks_ref[0].reshape(ROWS, WIDTH)
    for copy in (*rows[1], *rows[2]):
        copy.wait()


def weight_of(ref, shift):
    entries = ref[ROWS:ROWS + TAIL, 0:LANES].astype(F32)[2:3, :]
    return jnp.sum(jnp.where(iota((1, LANES), 1) == shift - 1, entries, 0.0), axis=1, keepdims=True)


def ids_row(ref):
    tail = ref[ROWS:ROWS + TAIL, :].astype(F32)
    return jnp.concatenate([tail[0:1, :], tail[1:2, 0:ROWS - WIDTH]], axis=1)


def tile_terms(scores, id_col, id_row, masked):
    rows, cols = scores.shape
    over_cols, over_rows = None, []
    for lane in range(cols // LANES):
        cut = slice(lane * LANES, (lane + 1) * LANES)
        half = jnp.tanh(scores[:, cut] * (0.5 * sharpness) - 0.5 * sharpness * threshold)
        factor = jnp.where(id_col == id_row[:, cut], 0.5, 0.25)
        term = factor * (1.0 + half)
        if masked:
            term = jnp.where(iota(term.shape, 0) == iota(term.shape, 1) + lane * LANES, 0.0, term)
        over_cols = term if over_cols is None else over_cols + term
        over_rows.append(jnp.sum(term.reshape(rows // 8, 8, LANES), axis=0))
    return over_cols, jnp.concatenate(over_rows, axis=1)


SIZE = 256
CUTS = [slice(at, at + SIZE) for at in range(0, ROWS, SIZE)]


def pair(a_ref, a_col, b_of, b_row, listed, row_acc, col_acc, total):
    @pl.when(jnp.sum(listed) > 0.0)
    def _():
        for part in CUTS:
            b = b_of(part)
            down = None
            for at in CUTS:
                by_row, by_col = tile_terms(nt(a_ref[at, :], b), a_col[at, :], b_row[:, part], False)
                row_acc[at, :] = row_acc[at, :] + by_row
                down = by_col if down is None else down + by_col
            col_acc[:, part] = down
        total[...] = total[...] + jnp.sum(col_acc[...], axis=0, keepdims=True)


def own_pair(ref, a_col, row, row_acc, col_acc):
    for i, at in enumerate(CUTS):
        a = ref[at, :]
        for j, part in enumerate(CUTS):
            if j < i:
                continue
            by_row, by_col = tile_terms(nt(a, ref[part, :]), a_col[at, :], row[:, part], i == j)
            row_acc[at, :] = row_acc[at, :] + by_row
            if j > i:
                col_acc[:, part] = col_acc[:, part] + by_col


def fold_rows(acc):
    return jnp.sum(jnp.transpose(acc[...]), axis=0, keepdims=True)


def first_kernel(own_ref, blocks_ref, ids_ref, sums_ref, col, row_acc, col_acc):
    col[...] = as_column(ids_ref[0])
    row_acc[...] = jnp.zeros_like(row_acc)
    sums_ref[...] = jnp.zeros_like(sums_ref)
    for c in range(1, COPIES):
        pair(
            own_ref, col, block_part(blocks_ref, c), ids_ref[c], weight_of(own_ref, APART * c), row_acc, col_acc,
            sums_ref.at[c],
        )
    sums_ref[0] = fold_rows(row_acc)


def self_kernel(own_ref, sum_ref, out_ref, col, row_acc, col_acc):
    row = ids_row(own_ref)
    col[...] = as_column(row)
    row_acc[...] = jnp.zeros_like(row_acc)
    col_acc[...] = jnp.zeros_like(col_acc)
    own_pair(own_ref, col, row, row_acc, col_acc)
    out_ref[...] = sum_ref[...] + fold_rows(row_acc) + jnp.sum(col_acc[...], axis=0, keepdims=True)


def block_part(blocks_ref, which):
    def part(rows):
        at = pl.ds(rows.start // PER_PAIR, SIZE // PER_PAIR)
        return blocks_ref[which, at, :, :].reshape(SIZE, WIDTH)

    return part


def second_kernel(core_ref, blocks_ref, ids_ref, sums_ref, sw_ref, *refs):
    outs, (total, col, row_acc, col_acc) = refs[:COPIES + 1], refs[COPIES + 1:]
    total[...] = sums_ref[...]
    col[...] = as_column(ids_row(sw_ref))
    row_acc[...] = jnp.zeros_like(row_acc)
    for n in range(2):
        which = 1 - core_ref[0] + n
        pair(
            sw_ref, col, block_part(blocks_ref, which), ids_ref[which], weight_of(sw_ref, 1 + 2 * n), row_acc,
            col_acc, total.at[which],
        )
    for c in range(COPIES):
        outs[c][...] = total[c]
    outs[COPIES][...] = fold_rows(row_acc)


def end_kernel(land_ref, *refs):
    out_ref = refs[-1]
    load = refs[0][...]
    for ref in refs[1:-1]:
        load = load + ref[...]
    result = 1.0 / (1.0 + load)
    high = result.astype(BF16).astype(F32)
    mid = (result - high).astype(BF16).astype(F32)
    low = result - high - mid
    which = iota((8, ROWS), 0)
    parts = jnp.where(which == 0, high, jnp.where(which == 1, mid, jnp.where(which == 2, low, 0.0))).astype(BF16)
    for step in range(4):
        placed = nt(parts, one_hot(256, step * 256, land_ref[...]))
        out_ref[:, step * 256:(step + 1) * 256] = placed[0:1, :] + placed[1:2, :] + placed[2:3, :]


def vec(n):
    return jax.ShapeDtypeStruct((1, n), F32)


def call(kernel, out_shape, in_specs, scratch, tasks, args, mib=40, out_spec=VMEM):
    single = not isinstance(out_shape, (list, tuple))
    return pl.pallas_call(
        kernel,
        out_shape=out_shape,
        in_specs=in_specs,
        out_specs=out_spec if single else [out_spec] * len(out_shape),
        scratch_shapes=scratch,
        compiler_params=pltpu.CompilerParams(vmem_limit_bytes=mib << 20),
        cost_estimate=pl.CostEstimate(
            flops=int(HINT * tasks * 2 * ROWS * ROWS * WIDTH),
            transcendentals=int(HINT * tasks * ROWS * ROWS),
            bytes_accessed=int(HINT * (1 + tasks) * 2 * ROWS * WIDTH),
        ),
    )(*args)


def move(value, devices, change, only=None):
    pairs = [
        (p, change(p))
        for p in range(devices)
        if 0 <= change(p) < devices and (only is None or p % 2 == only)
    ]
    return lax.ppermute(value, AXES, pairs)


def local(embeddings, sorted_slot, cluster_ids, block_list):
    devices = lax.axis_size(AXES)
    position = lax.axis_index(AXES)
    core = (position % 2).astype(jnp.int32).reshape(1)
    move_d = functools.partial(move, devices=devices)
    scratch = pltpu.VMEM

    outgoing = call(
        functools.partial(front_kernel, devices),
        jax.ShapeDtypeStruct((devices * MESSAGE, LANES), BF16), [ANY] * 2,
        [scratch((1, ROWS), jnp.int32), scratch((ROWS, WIDTH), BF16), scratch((ROWS, WIDTH + LANES), BF16)]
        + [scratch((ROWS, LANES), BF16), scratch((devices * MESSAGE, LANES), BF16), pltpu.SemaphoreType.DMA((5,))],
        1, (sorted_slot.reshape(1, ROWS), embeddings), 62, ANY,
    )
    arrived = lax.all_to_all(outgoing, AXES, split_axis=0, concat_axis=0, tiled=True)
    got = arrived.reshape(devices, MESSAGE, LANES)
    ids = cluster_ids.reshape(1, ROWS)
    far_ids = [move_d(ids, change=lambda p, c=c: p - APART * c) for c in range(1, COPIES)]
    reach = position + 1 + jnp.arange(SHIFTS, dtype=jnp.int32)
    entries = jnp.pad(jnp.where(reach[None, :] < devices, block_list, 0), ((0, 0), (0, LANES - SHIFTS)))
    tile_rows = lambda width: pltpu.VMEM((devices, PER_PAIR, width), BF16)
    sems = pltpu.SemaphoreType.DMA
    own, blocks, block_ids, land = call(
        split_kernel,
        [
            jax.ShapeDtypeStruct((ROWS + TAIL, WIDTH), BF16),
            jax.ShapeDtypeStruct((COPIES, devices, PER_PAIR, WIDTH), BF16),
            jax.ShapeDtypeStruct((COPIES, 1, ROWS), F32),
            jax.ShapeDtypeStruct((1, ROWS), jnp.int32),
        ],
        [ANY] + [VMEM] * (1 + COPIES), [tile_rows(LANES), sems((COPIES, PIECES + 1))],
        0.5, (got, entries, ids, *far_ids), 16,
    )
    sw = move_d(own, change=lambda p: p ^ 1)
    sides = [scratch((ROWS, LANES), F32)] * 2 + [scratch((8, ROWS), F32)]
    sums = call(
        first_kernel, jax.ShapeDtypeStruct((COPIES, 1, ROWS), F32), [VMEM] * 3, sides, 2, (own, blocks, block_ids), 16
    )
    sums = call(
        second_kernel, [vec(ROWS)] * (COPIES + 1), [SMEM] + [VMEM] * 4,
        [scratch((COPIES, 1, ROWS), F32)] + sides,
        2, (core, blocks, block_ids, sums, sw), 16,
    )
    own_sum = call(
        self_kernel, vec(ROWS), [VMEM] * 2, sides,
        0.6, (own, sums[0]), 16,
    )
    returned = [own_sum, move_d(sums[COPIES], change=lambda p: p ^ 1)]
    returned += [move_d(sums[c], change=lambda p, c=c: p + APART * c) for c in range(1, COPIES)]
    weights = call(end_kernel, vec(ROWS), [VMEM] * (COPIES + 2), [], 0.2, (land, *returned))
    return weights.reshape(ROWS)


def solution(mesh):
    in_specs = (
        P(("grp", "gr", "gc"), None),
        P(("grp", "gr", "gc")),
        P(("grp", "gr", "gc")),
        P(("grp", "gr", "gc"), None),
    )
    out_specs = P(("grp", "gr", "gc"))
    return jax.shard_map(local, mesh=mesh, in_specs=in_specs, out_specs=out_specs, check_vma=False)
```

profile of v0, /device:TPU:34, one launch (start us, length us, event | category | flops | bytes accessed | tf_op | source)
XLA Modules:
  0.0 103.4 jit_solution(6447876794056543872)
XLA Ops:
  0.0 5.2 %shard_map.46 = bf16[19456,128]{1,0:T(8,128)(2,1)} custom-call(s32[1,1024]{1,0:T(1,128)} %bitcast.9, bf16[1024,768]{1,0:T(8,128)(2,1)} %emb_ref.1), custom_call_target="tpu_custom_call" | custom-call | flops 32212254720 | bytes 62914560 | tf_op jit(solution)/shard_map/pallas_call | solution.py:301
  5.2 0.0 copy-start
  5.2 0.0 copy-start.1
  5.2 10.4 %all-to-all-start = ((bf16[64,304,128]{2,1,0:T(8,128)(2,1)}), bf16[64,304,128]{2,1,0:T(8,128)(2,1)}, u32[]{:S(2)}, u32[]{:S(2)}) async-start(bf16[64,304,128]{2,1,0:T(8,128)(2,1)} %bitcast.8), calls=%async_computation | async-start | bytes 9961472 | tf_op jit(solution)/shard_map/all_to_all | solution.py:339
  15.6 0.0 copy-done
  15.6 7.3 %collective-permute-start.1 = (s32[1,1024]{1,0:T(1,128)S(1)}, s32[1,1024]{1,0:T(1,128)S(1)}, u32[]{:S(2)}, u32[]{:S(2)}) collective-permute-start(s32[1,1024]{1,0:T(1,128)S(1)} %bitcast.5), channel_id=1, source_target_pairs={{4,0},{5,1},{6,2},{7,3},{8,4},{9,5},{10,6},{11,7},{12,8},{13,9},{1... | collective-permute-start | bytes 12296 | tf_op jit(solution)/shard_map/ppermute | solution.py:322
  22.9 3.1 %collective-permute-start = (s32[1,1024]{1,0:T(1,128)S(1)}, s32[1,1024]{1,0:T(1,128)S(1)}, u32[]{:S(2)}, u32[]{:S(2)}) collective-permute-start(s32[1,1024]{1,0:T(1,128)S(1)} %bitcast.6), channel_id=1, source_target_pairs={{2,0},{3,1},{4,2},{5,3},{6,4},{7,5},{8,6},{9,7},{10,8},{11,9},{12,... | collective-permute-start | bytes 12296 | tf_op jit(solution)/shard_map/ppermute | solution.py:322
  26.0 0.0 copy-done.1
  26.0 45.1 %collective-permute-done.1.refs_2_ = s32[1,1024]{1,0:T(1,128)S(1)} collective-permute-done((s32[1,1024]{1,0:T(1,128)S(1)}, s32[1,1024]{1,0:T(1,128)S(1)}, u32[]{:S(2)}, u32[]{:S(2)}) %collective-permute-start.1) | collective-permute-done | bytes 4128 | tf_op jit(solution)/shard_map/ppermute | solution.py:322
  71.1 0.0 collective-permute-done.refs_1_
  71.1 3.8 %all-to-all-done.got_hbm = bf16[64,304,128]{2,1,0:T(8,128)(2,1)} async-done(((bf16[64,304,128]{2,1,0:T(8,128)(2,1)}), bf16[64,304,128]{2,1,0:T(8,128)(2,1)}, u32[]{:S(2)}, u32[]{:S(2)}) %all-to-all-start) | async-done | bytes 4980768 | tf_op jit(solution)/shard_map/all_to_all | solution.py:339
  74.9 2.6 %shard_map.47 = (bf16[1040,768]{1,0:T(8,128)(2,1)S(1)}, bf16[3,64,16,768]{3,2,1,0:T(8,128)(2,1)S(1)}, f32[3,1,1024]{2,1,0:T(1,128)S(1)}, s32[1,1024]{1,0:T(1,128)S(1)}) custom-call(bf16[64,304,128]{2,1,0:T(8,128)(2,1)} %all-to-all-done.got_hbm, s32[1,128]{1,0:T(1,128)S(1)} %pad.4.list_ref, s32[1,1024]{1,0:T(1,128)S(1)} %bitcast.7, ...), custom_call_target="tpu_custom_call" | custom-call | flops 16106127360 | bytes 47185920 | tf_op jit(solution)/shard_map/pallas_call | solution.py:301
  77.6 2.1 %collective-permute-start.2 = (bf16[1040,768]{1,0:T(8,128)(2,1)S(1)}, bf16[1040,768]{1,0:T(8,128)(2,1)S(1)}, u32[]{:S(2)}, u32[]{:S(2)}) collective-permute-start(bf16[1040,768]{1,0:T(8,128)(2,1)S(1)} %get-tuple-element.14.own_ref), channel_id=1, source_target_pairs={{0,1},{1,0},{2,3},{3,2},{4,5},{5,4},{6,7},{7,6},{8,9},{9,8},{10,11... | collective-permute-start | bytes 4792328 | tf_op jit(solution)/shard_map/ppermute | solution.py:322
  79.7 2.7 %shard_map.48.sums_ref = f32[3,1,1024]{2,1,0:T(1,128)S(1)} custom-call(bf16[1040,768]{1,0:T(8,128)(2,1)S(1)} %get-tuple-element.14.own_ref, bf16[3,64,16,768]{3,2,1,0:T(8,128)(2,1)S(1)} %get-tuple-element.15.blocks_ref, f32[3,1,1024]{2,1,0:T(1,128)S(1)} %get-tuple-element.16.ids_ref), custom_call_target="tpu_custom_call" | custom-call | flops 64424509440 | bytes 94371840 | tf_op jit(solution)/shard_map/pallas_call | solution.py:301
  82.4 0.4 collective-permute-done.2.sw_ref
  82.7 2.8 %shard_map.49 = (f32[1,1024]{1,0:T(1,128)S(1)}, f32[1,1024]{1,0:T(1,128)S(1)}, f32[1,1024]{1,0:T(1,128)S(1)}, f32[1,1024]{1,0:T(1,128)S(1)}) custom-call(s32[1]{0:T(128)} %bitcast.3.core_ref, bf16[3,64,16,768]{3,2,1,0:T(8,128)(2,1)S(1)} %get-tuple-element.15.blocks_ref, f32[3,1,1024]{2,1,0:T(1,128)S(1)} %get-tuple-element.16.ids_ref, ...), custom_call_target="tpu_custom_call" | custom-call | flops 64424509440 | bytes 94371840 | tf_op jit(solution)/shard_map/pallas_call | solution.py:301
  85.6 0.4 collective-permute-start.3
  86.0 5.8 %collective-permute-start.4 = (f32[1,1024]{1,0:T(1,128)S(1)}, f32[1,1024]{1,0:T(1,128)S(1)}, u32[]{:S(2)}, u32[]{:S(2)}) collective-permute-start(f32[1,1024]{1,0:T(1,128)S(1)} %get-tuple-element.19), channel_id=1, source_target_pairs={{0,2},{1,3},{2,4},{3,5},{4,6},{5,7},{6,8},{7,9},{8,10},{9,11},{10,... | collective-permute-start | bytes 12296 | tf_op jit(solution)/shard_map/ppermute | solution.py:322
  91.9 1.9 %collective-permute-start.5 = (f32[1,1024]{1,0:T(1,128)S(1)}, f32[1,1024]{1,0:T(1,128)S(1)}, u32[]{:S(2)}, u32[]{:S(2)}) collective-permute-start(f32[1,1024]{1,0:T(1,128)S(1)} %get-tuple-element.20), channel_id=1, source_target_pairs={{0,4},{1,5},{2,6},{3,7},{4,8},{5,9},{6,10},{7,11},{8,12},{9,13},{1... | collective-permute-start | bytes 12296 | tf_op jit(solution)/shard_map/ppermute | solution.py:322
  93.8 1.5 %shard_map.50.refs_0_ = f32[1,1024]{1,0:T(1,128)S(1)} custom-call(bf16[1040,768]{1,0:T(8,128)(2,1)S(1)} %get-tuple-element.14.own_ref, f32[1,1024]{1,0:T(1,128)S(1)} %get-tuple-element.17.sum_ref), custom_call_target="tpu_custom_call" | custom-call | flops 19327352832 | bytes 50331648 | tf_op jit(solution)/shard_map/pallas_call | solution.py:301
  95.3 0.0 collective-permute-done.3.refs_1_
  95.3 0.7 collective-permute-done.4.refs_2_
  96.0 6.2 %collective-permute-done.5.refs_3_ = f32[1,1024]{1,0:T(1,128)S(1)} collective-permute-done((f32[1,1024]{1,0:T(1,128)S(1)}, f32[1,1024]{1,0:T(1,128)S(1)}, u32[]{:S(2)}, u32[]{:S(2)}) %collective-permute-start.5) | collective-permute-done | bytes 4128 | tf_op jit(solution)/shard_map/ppermute | solution.py:322
  102.2 1.3 %shard_map.51 = f32[1,1024]{1,0:T(1,128)} custom-call(s32[1,1024]{1,0:T(1,128)S(1)} %get-tuple-element.13.land_ref, f32[1,1024]{1,0:T(1,128)S(1)} %shard_map.50.refs_0_, f32[1,1024]{1,0:T(1,128)S(1)} %collective-permute-done.3.refs_1_, f32[1,1024]{1,0:T(1,128)S(1)} %collective-permute-done.4.refs_2_, f32[1,1024]{1,0:T(1,128)S(1)} %collective-permute-done.5.refs_3_), custom_call_target="tpu_custom_call" | custom-call | flops 6442450944 | bytes 37748736 | tf_op jit(solution)/shard_map/pallas_call | solution.py:301
  (2 shorter events, 0.0 us)
Async XLA Ops:
  5.2 10.4 %copy-start = (s32[1024]{0:T(1024)S(1)}, s32[1024]{0:T(1024)}, u32[]{:S(2)}) copy-start(s32[1024]{0:T(1024)} %param.6) | copy-start | bytes 12292
  5.2 20.8 %copy-start.1 = (s32[1,4]{1,0:T(1,128)S(1)}, s32[1,4]{1,0:T(1,128)}, u32[]{:S(2)}) copy-start(s32[1,4]{1,0:T(1,128)} %param.7) | copy-start | bytes 52
  5.2 69.7 %all-to-all-start = ((bf16[64,304,128]{2,1,0:T(8,128)(2,1)}), bf16[64,304,128]{2,1,0:T(8,128)(2,1)}, u32[]{:S(2)}, u32[]{:S(2)}) async-start(bf16[64,304,128]{2,1,0:T(8,128)(2,1)} %bitcast.8), calls=%async_computation | async-start | bytes 9961472 | tf_op jit(solution)/shard_map/all_to_all | solution.py:339
  15.6 55.5 %collective-permute-start.1 = (s32[1,1024]{1,0:T(1,128)S(1)}, s32[1,1024]{1,0:T(1,128)S(1)}, u32[]{:S(2)}, u32[]{:S(2)}) collective-permute-start(s32[1,1024]{1,0:T(1,128)S(1)} %bitcast.5), channel_id=1, source_target_pairs={{4,0},{5,1},{6,2},{7,3},{8,4},{9,5},{10,6},{11,7},{12,8},{13,9},{1... | collective-permute-start | bytes 12296 | tf_op jit(solution)/shard_map/ppermute | solution.py:322
  22.9 48.2 %collective-permute-start = (s32[1,1024]{1,0:T(1,128)S(1)}, s32[1,1024]{1,0:T(1,128)S(1)}, u32[]{:S(2)}, u32[]{:S(2)}) collective-permute-start(s32[1,1024]{1,0:T(1,128)S(1)} %bitcast.6), channel_id=1, source_target_pairs={{2,0},{3,1},{4,2},{5,3},{6,4},{7,5},{8,6},{9,7},{10,8},{11,9},{12,... | collective-permute-start | bytes 12296 | tf_op jit(solution)/shard_map/ppermute | solution.py:322
  77.6 5.1 %collective-permute-start.2 = (bf16[1040,768]{1,0:T(8,128)(2,1)S(1)}, bf16[1040,768]{1,0:T(8,128)(2,1)S(1)}, u32[]{:S(2)}, u32[]{:S(2)}) collective-permute-start(bf16[1040,768]{1,0:T(8,128)(2,1)S(1)} %get-tuple-element.14.own_ref), channel_id=1, source_target_pairs={{0,1},{1,0},{2,3},{3,2},{4,5},{5,4},{6,7},{7,6},{8,9},{9,8},{10,11... | collective-permute-start | bytes 4792328 | tf_op jit(solution)/shard_map/ppermute | solution.py:322
  85.6 9.7 %collective-permute-start.3 = (f32[1,1024]{1,0:T(1,128)S(1)}, f32[1,1024]{1,0:T(1,128)S(1)}, u32[]{:S(2)}, u32[]{:S(2)}) collective-permute-start(f32[1,1024]{1,0:T(1,128)S(1)} %get-tuple-element.18), channel_id=1, source_target_pairs={{0,1},{1,0},{2,3},{3,2},{4,5},{5,4},{6,7},{7,6},{8,9},{9,8},{10,11... | collective-permute-start | bytes 12296 | tf_op jit(solution)/shard_map/ppermute | solution.py:322
  86.0 10.0 %collective-permute-start.4 = (f32[1,1024]{1,0:T(1,128)S(1)}, f32[1,1024]{1,0:T(1,128)S(1)}, u32[]{:S(2)}, u32[]{:S(2)}) collective-permute-start(f32[1,1024]{1,0:T(1,128)S(1)} %get-tuple-element.19), channel_id=1, source_target_pairs={{0,2},{1,3},{2,4},{3,5},{4,6},{5,7},{6,8},{7,9},{8,10},{9,11},{10,... | collective-permute-start | bytes 12296 | tf_op jit(solution)/shard_map/ppermute | solution.py:322
  91.9 10.3 %collective-permute-start.5 = (f32[1,1024]{1,0:T(1,128)S(1)}, f32[1,1024]{1,0:T(1,128)S(1)}, u32[]{:S(2)}, u32[]{:S(2)}) collective-permute-start(f32[1,1024]{1,0:T(1,128)S(1)} %get-tuple-element.20), channel_id=1, source_target_pairs={{0,4},{1,5},{2,6},{3,7},{4,8},{5,9},{6,10},{7,11},{8,12},{9,13},{1... | collective-permute-start | bytes 12296 | tf_op jit(solution)/shard_map/ppermute | solution.py:322
where the time goes:
time: 104 us; the launch traced here: 103 us
  waiting for transfers between devices  56.2 us (54%)
  starting transfers between devices  31 us (30%)
  Pallas kernels  16.1 us (15%)
    ppermute x6, waiting for transfers between devices, move(): return lax.ppermute(value, AXES, pairs)  52.3 us
    ppermute x6, starting transfers between devices, move(): return lax.ppermute(value, AXES, pairs)  20.6 us
    pallas_call x6, Pallas kernels, call(): pl.pallas_call(kernel, out_shape=out_shape, in_specs=in_specs, out_specs=...  16.1 us
    all_to_all x1, starting transfers between devices, local(): lax.all_to_all(outgoing, AXES, split_axis=0, concat_axis=0, tiled=True)  10.4 us
    all_to_all x1, waiting for transfers between devices, local(): lax.all_to_all(outgoing, AXES, split_axis=0, concat_axis=0, tiled=True)  3.84 us
  transfers between devices with their start and end apart: 7, of which 5 were waited for; matrix products, arithmetic and copies ran while one was open for 0% of the time, Pallas kernels for 4%

commit v1 on v0

--- a/solution.py
+++ b/solution.py
@@ -17,7 +17,9 @@
 APART = 2
 PER_PAIR = 16
 PIECES = WIDTH // LANES
-MESSAGE = (COPIES * PIECES + 1) * PER_PAIR
+BODY = PIECES * PER_PAIR
+HALF = PER_PAIR // 2
+MESSAGE = COPIES * BODY + HALF
 TAIL = 16
 DIGITS = 32
 AXES = ("gr", "gc")
@@ -49,7 +51,7 @@
     return jnp.transpose(jnp.broadcast_to(row, (LANES, row.shape[1])))
 
 
-def front_kernel(devices, slot_hbm, emb_ref, out_hbm, slot_ref, raw_ref, unit_ref, digit_ref, out_ref, sems):
+def front_kernel(devices, slot_hbm, emb_ref, out_hbm, slot_ref, raw_ref, unit_ref, digit_ref, info_ref, rows_ref, sems):
     size = 256
     parts = [pl.ds(at, size) for at in range(0, ROWS, size)]
     slots = pltpu.make_async_copy(slot_hbm, slot_ref, sems.at[len(parts)])
@@ -83,38 +85,40 @@
         mean = jnp.sum(values * values, axis=1, keepdims=True) * (1.0 / WIDTH)
         inverse = lax.rsqrt(mean + 1e-06) * (1.0 / math.sqrt(WIDTH))
         unit_ref[part, 0:WIDTH] = (values * inverse).astype(BF16)
-    reach = APART * (COPIES - 1)
     per_part = size // PER_PAIR
     back = []
 
-    def send(first, count):
-        for device in range(first, first + count):
-            tile = digit_ref[device * PER_PAIR:(device + 1) * PER_PAIR, :]
-            for copy in range(1, COPIES):
-                at = (device + APART * copy) % devices * PER_PAIR
-                tile = jnp.where(lane == copy, digit_ref[at:at + PER_PAIR, :], tile)
-            out_ref[(device + 1) * MESSAGE - PER_PAIR:(device + 1) * MESSAGE, :] = tile
-        rows = pl.ds(first * MESSAGE, count * MESSAGE)
-        back.append(pltpu.make_async_copy(out_ref.at[rows, :], out_hbm.at[rows, :], sems.at[len(back)]))
+    def send(source, target):
+        back.append(pltpu.make_async_copy(source, target, sems.at[len(parts) + 1 + len(back)]))
         back[-1].start()
 
-    lane = iota((PER_PAIR, LANES), 1) // 2
+    lane = iota((per_part, HALF, LANES), 2)
     for n, part in enumerate(parts):
         place = one_hot(size, n * size, dest)
-        placed = jnp.dot(place, unit_ref[...], preferred_element_type=F32).astype(BF16)
-        digit_ref[part, :] = placed[:, WIDTH:]
+        placed = jnp.dot(place, unit_ref[...], preferred_element_type=F32)
+        first = n * per_part
+        sent = placed[:, WIDTH:].reshape(per_part, PER_PAIR, LANES)
+        digit_ref[first:first + per_part] = jnp.where(lane < LANES // 2, sent[:, 0:HALF, :], sent[:, HALF:, :])
         for i in range(per_part):
-            block = n * per_part + i
-            rows = placed[i * PER_PAIR:(i + 1) * PER_PAIR, :]
-            for copy in range(COPIES):
-                at = (block - APART * copy) % devices * MESSAGE + copy * PIECES * PER_PAIR
-                for piece in range(PIECES):
-                    out_ref[at + piece * PER_PAIR:at + (piece + 1) * PER_PAIR, :] = rows[:, piece * LANES:(piece + 1) * LANES]
-        if n == 0:
-            send(0, per_part - reach)
-        else:
-            send(n * per_part - reach, per_part)
-    send(devices - reach, reach)
+            rows = placed[i * PER_PAIR:(i + 1) * PER_PAIR, :].astype(BF16)
+            for piece in range(PIECES):
+                rows_ref[first + i, piece * PER_PAIR:(piece + 1) * PER_PAIR, :] = rows[:, piece * LANES:(piece + 1) * LANES]
+        for copy in range(COPIES):
+            back_by = APART * copy
+            body = pl.ds(copy * BODY, BODY)
+            wrapped = max(0, back_by - first)
+            if wrapped:
+                send(rows_ref.at[pl.ds(first, wrapped)], out_hbm.at[pl.ds(devices - wrapped, wrapped), body, :])
+            count = per_part - wrapped
+            send(rows_ref.at[pl.ds(first + wrapped, count)], out_hbm.at[pl.ds(first + wrapped - back_by, count), body, :])
+    which = iota((devices, HALF, LANES), 2) % (LANES // 2) // 2
+    info = digit_ref[...]
+    for copy in range(1, COPIES):
+        ahead = APART * copy
+        far = jnp.concatenate([digit_ref[ahead:], digit_ref[:ahead]], axis=0)
+        info = jnp.where(which == copy, far, info)
+    info_ref[...] = info.astype(BF16)
+    send(info_ref, out_hbm.at[:, pl.ds(COPIES * BODY, HALF), :])
     for copy in back:
         copy.wait()
 
@@ -130,13 +134,16 @@
 
 
 def slot_tiles(got_hbm, target, sem):
-    copy = pltpu.make_async_copy(got_hbm.at[:, pl.ds(MESSAGE - PER_PAIR, PER_PAIR), :], target, sem)
+    copy = pltpu.make_async_copy(got_hbm.at[:, pl.ds(COPIES * BODY, HALF), :], target, sem)
     copy.start()
     return copy
 
 
 def arrival_slots(digits, copies):
-    digits = jnp.transpose(digits.reshape(ROWS, LANES).astype(F32))[0:8, :]
+    upper = digits.astype(F32)
+    lower = jnp.concatenate([upper[:, :, LANES // 2:], upper[:, :, :LANES // 2]], axis=2)
+    digits = jnp.concatenate([upper, lower], axis=1).reshape(ROWS, LANES)
+    digits = jnp.transpose(digits)[0:8, :]
     return [(digits[2 * c:2 * c + 1, :] * DIGITS + digits[2 * c + 1:2 * c + 2, :]).astype(jnp.int32) for c in copies]
 
 
@@ -331,18 +338,17 @@
 
     outgoing = call(
         functools.partial(front_kernel, devices),
-        jax.ShapeDtypeStruct((devices * MESSAGE, LANES), BF16), [ANY] * 2,
+        jax.ShapeDtypeStruct((devices, MESSAGE, LANES), BF16), [ANY] * 2,
         [scratch((1, ROWS), jnp.int32), scratch((ROWS, WIDTH), BF16), scratch((ROWS, WIDTH + LANES), BF16)]
-        + [scratch((ROWS, LANES), BF16), scratch((devices * MESSAGE, LANES), BF16), pltpu.SemaphoreType.DMA((5,))],
+        + [scratch((devices, HALF, LANES), F32), scratch((devices, HALF, LANES), BF16)]
+        + [scratch((devices, BODY, LANES), BF16), pltpu.SemaphoreType.DMA((24,))],
         1, (sorted_slot.reshape(1, ROWS), embeddings), 62, ANY,
     )
-    arrived = lax.all_to_all(outgoing, AXES, split_axis=0, concat_axis=0, tiled=True)
-    got = arrived.reshape(devices, MESSAGE, LANES)
+    got = lax.all_to_all(outgoing, AXES, split_axis=0, concat_axis=0, tiled=True)
     ids = cluster_ids.reshape(1, ROWS)
     far_ids = [move_d(ids, change=lambda p, c=c: p - APART * c) for c in range(1, COPIES)]
     reach = position + 1 + jnp.arange(SHIFTS, dtype=jnp.int32)
     entries = jnp.pad(jnp.where(reach[None, :] < devices, block_list, 0), ((0, 0), (0, LANES - SHIFTS)))
-    tile_rows = lambda width: pltpu.VMEM((devices, PER_PAIR, width), BF16)
     sems = pltpu.SemaphoreType.DMA
     own, blocks, block_ids, land = call(
         split_kernel,
@@ -352,7 +358,7 @@
             jax.ShapeDtypeStruct((COPIES, 1, ROWS), F32),
             jax.ShapeDtypeStruct((1, ROWS), jnp.int32),
         ],
-        [ANY] + [VMEM] * (1 + COPIES), [tile_rows(LANES), sems((COPIES, PIECES + 1))],
+        [ANY] + [VMEM] * (1 + COPIES), [scratch((devices, HALF, LANES), BF16), sems((COPIES, PIECES + 1))],
         0.5, (got, entries, ids, *far_ids), 16,
     )
     sw = move_d(own, change=lambda p: p ^ 1)

time: 104 us -> 104 us (level)
  Pallas kernels: 16.1 us -> 14 us
  starting transfers between devices: 31 us -> 32.2 us
    pallas_call x6, Pallas kernels: 16.1 us -> 14 us  [call(): pl.pallas_call(kernel, out_shape=out_shape, in_specs=in_specs, out_specs=...]
    ppermute x6, starting transfers between devices: 20.6 us -> 21.9 us  [move(): return lax.ppermute(value, AXES, pairs)]
  transfers between devices with their start and end apart: 7 -> 7, of which waited for: 5 -> 5; matrix products, arithmetic and copies ran while one was open for 0% -> 0% of each run, Pallas kernels for 4% -> 2%
where the time goes in v1:
time: 104 us; the launch traced here: 103 us
  waiting for transfers between devices  56.9 us (55%)
  starting transfers between devices  32.2 us (31%)
  Pallas kernels  14 us (13%)
    ppermute x6, waiting for transfers between devices, move(): return lax.ppermute(value, AXES, pairs)  53.1 us
    ppermute x6, starting transfers between devices, move(): return lax.ppermute(value, AXES, pairs)  21.9 us
    pallas_call x6, Pallas kernels, call(): pl.pallas_call(kernel, out_shape=out_shape, in_specs=in_specs, out_specs=...  14 us
    all_to_all x1, starting transfers between devices, local(): lax.all_to_all(outgoing, AXES, split_axis=0, concat_axis=0, tiled=True)  10.4 us
    all_to_all x1, waiting for transfers between devices, local(): lax.all_to_all(outgoing, AXES, split_axis=0, concat_axis=0, tiled=True)  3.85 us
  transfers between devices with their start and end apart: 7, of which 5 were waited for; matrix products, arithmetic and copies ran while one was open for 0% of the time, Pallas kernels for 2%

profile of v1, /device:TPU:34, one launch (start us, length us, event | category | flops | bytes accessed | tf_op | source)
XLA Modules:
  0.0 103.3 jit_solution(12009650671370270844)
XLA Ops:
  0.0 5.2 %shard_map.46 = bf16[64,296,128]{2,1,0:T(8,128)(2,1)} custom-call(s32[1,1024]{1,0:T(1,128)} %bitcast.7, bf16[1024,768]{1,0:T(8,128)(2,1)} %emb_ref.1), custom_call_target="tpu_custom_call" | custom-call | flops 32212254720 | bytes 62914560 | tf_op jit(solution)/shard_map/pallas_call | solution.py:308
  5.3 0.0 copy-start
  5.3 0.0 copy-start.1
  5.3 10.4 %all-to-all-start = ((bf16[64,296,128]{2,1,0:T(8,128)(2,1)}), bf16[64,296,128]{2,1,0:T(8,128)(2,1)}, u32[]{:S(2)}, u32[]{:S(2)}) async-start(bf16[64,296,128]{2,1,0:T(8,128)(2,1)} %shard_map.46), calls=%async_computation | async-start | bytes 9699328 | tf_op jit(solution)/shard_map/all_to_all | solution.py:347
  15.6 0.0 copy-done
  15.6 7.3 %collective-permute-start.1 = (s32[1,1024]{1,0:T(1,128)S(1)}, s32[1,1024]{1,0:T(1,128)S(1)}, u32[]{:S(2)}, u32[]{:S(2)}) collective-permute-start(s32[1,1024]{1,0:T(1,128)S(1)} %bitcast.4), channel_id=1, source_target_pairs={{4,0},{5,1},{6,2},{7,3},{8,4},{9,5},{10,6},{11,7},{12,8},{13,9},{1... | collective-permute-start | bytes 12296 | tf_op jit(solution)/shard_map/ppermute | solution.py:329
  22.9 3.1 %collective-permute-start = (s32[1,1024]{1,0:T(1,128)S(1)}, s32[1,1024]{1,0:T(1,128)S(1)}, u32[]{:S(2)}, u32[]{:S(2)}) collective-permute-start(s32[1,1024]{1,0:T(1,128)S(1)} %bitcast.5), channel_id=1, source_target_pairs={{2,0},{3,1},{4,2},{5,3},{6,4},{7,5},{8,6},{9,7},{10,8},{11,9},{12,... | collective-permute-start | bytes 12296 | tf_op jit(solution)/shard_map/ppermute | solution.py:329
  26.0 0.0 copy-done.1
  26.1 43.7 %collective-permute-done.1.refs_2_ = s32[1,1024]{1,0:T(1,128)S(1)} collective-permute-done((s32[1,1024]{1,0:T(1,128)S(1)}, s32[1,1024]{1,0:T(1,128)S(1)}, u32[]{:S(2)}, u32[]{:S(2)}) %collective-permute-start.1) | collective-permute-done | bytes 4128 | tf_op jit(solution)/shard_map/ppermute | solution.py:329
  69.8 0.0 collective-permute-done.refs_1_
  69.8 3.9 %all-to-all-done.got_hbm = bf16[64,296,128]{2,1,0:T(8,128)(2,1)} async-done(((bf16[64,296,128]{2,1,0:T(8,128)(2,1)}), bf16[64,296,128]{2,1,0:T(8,128)(2,1)}, u32[]{:S(2)}, u32[]{:S(2)}) %all-to-all-start) | async-done | bytes 4849696 | tf_op jit(solution)/shard_map/all_to_all | solution.py:347
  73.6 2.6 %shard_map.47 = (bf16[1040,768]{1,0:T(8,128)(2,1)S(1)}, bf16[3,64,16,768]{3,2,1,0:T(8,128)(2,1)S(1)}, f32[3,1,1024]{2,1,0:T(1,128)S(1)}, s32[1,1024]{1,0:T(1,128)S(1)}) custom-call(bf16[64,296,128]{2,1,0:T(8,128)(2,1)} %all-to-all-done.got_hbm, s32[1,128]{1,0:T(1,128)S(1)} %pad.4.list_ref, s32[1,1024]{1,0:T(1,128)S(1)} %bitcast.6, ...), custom_call_target="tpu_custom_call" | custom-call | flops 16106127360 | bytes 47185920 | tf_op jit(solution)/shard_map/pallas_call | solution.py:308
  76.3 2.0 %collective-permute-start.2 = (bf16[1040,768]{1,0:T(8,128)(2,1)S(1)}, bf16[1040,768]{1,0:T(8,128)(2,1)S(1)}, u32[]{:S(2)}, u32[]{:S(2)}) collective-permute-start(bf16[1040,768]{1,0:T(8,128)(2,1)S(1)} %get-tuple-element.14.own_ref), channel_id=1, source_target_pairs={{0,1},{1,0},{2,3},{3,2},{4,5},{5,4},{6,7},{7,6},{8,9},{9,8},{10,11... | collective-permute-start | bytes 4792328 | tf_op jit(solution)/shard_map/ppermute | solution.py:329
  78.2 0.6 shard_map.48.sums_ref
  78.8 2.5 %collective-permute-done.2.sw_ref = bf16[1040,768]{1,0:T(8,128)(2,1)S(1)} collective-permute-done((bf16[1040,768]{1,0:T(8,128)(2,1)S(1)}, bf16[1040,768]{1,0:T(8,128)(2,1)S(1)}, u32[]{:S(2)}, u32[]{:S(2)}) %collective-permute-start.2) | collective-permute-done | bytes 1597472 | tf_op jit(solution)/shard_map/ppermute | solution.py:329
  81.3 2.8 %shard_map.49 = (f32[1,1024]{1,0:T(1,128)S(1)}, f32[1,1024]{1,0:T(1,128)S(1)}, f32[1,1024]{1,0:T(1,128)S(1)}, f32[1,1024]{1,0:T(1,128)S(1)}) custom-call(s32[1]{0:T(128)} %bitcast.2.core_ref, bf16[3,64,16,768]{3,2,1,0:T(8,128)(2,1)S(1)} %get-tuple-element.15.blocks_ref, f32[3,1,1024]{2,1,0:T(1,128)S(1)} %get-tuple-element.16.ids_ref, ...), custom_call_target="tpu_custom_call" | custom-call | flops 64424509440 | bytes 94371840 | tf_op jit(solution)/shard_map/pallas_call | solution.py:308
  84.1 2.5 %collective-permute-start.3 = (f32[1,1024]{1,0:T(1,128)S(1)}, f32[1,1024]{1,0:T(1,128)S(1)}, u32[]{:S(2)}, u32[]{:S(2)}) collective-permute-start(f32[1,1024]{1,0:T(1,128)S(1)} %get-tuple-element.18), channel_id=1, source_target_pairs={{0,1},{1,0},{2,3},{3,2},{4,5},{5,4},{6,7},{7,6},{8,9},{9,8},{10,11... | collective-permute-start | bytes 12296 | tf_op jit(solution)/shard_map/ppermute | solution.py:329
  86.6 5.1 %collective-permute-start.4 = (f32[1,1024]{1,0:T(1,128)S(1)}, f32[1,1024]{1,0:T(1,128)S(1)}, u32[]{:S(2)}, u32[]{:S(2)}) collective-permute-start(f32[1,1024]{1,0:T(1,128)S(1)} %get-tuple-element.19), channel_id=1, source_target_pairs={{0,2},{1,3},{2,4},{3,5},{4,6},{5,7},{6,8},{7,9},{8,10},{9,11},{10,... | collective-permute-start | bytes 12296 | tf_op jit(solution)/shard_map/ppermute | solution.py:329
  91.8 1.9 %collective-permute-start.5 = (f32[1,1024]{1,0:T(1,128)S(1)}, f32[1,1024]{1,0:T(1,128)S(1)}, u32[]{:S(2)}, u32[]{:S(2)}) collective-permute-start(f32[1,1024]{1,0:T(1,128)S(1)} %get-tuple-element.20), channel_id=1, source_target_pairs={{0,4},{1,5},{2,6},{3,7},{4,8},{5,9},{6,10},{7,11},{8,12},{9,13},{1... | collective-permute-start | bytes 12296 | tf_op jit(solution)/shard_map/ppermute | solution.py:329
  93.7 1.5 %shard_map.50.refs_0_ = f32[1,1024]{1,0:T(1,128)S(1)} custom-call(bf16[1040,768]{1,0:T(8,128)(2,1)S(1)} %get-tuple-element.14.own_ref, f32[1,1024]{1,0:T(1,128)S(1)} %get-tuple-element.17.sum_ref), custom_call_target="tpu_custom_call" | custom-call | flops 19327352832 | bytes 50331648 | tf_op jit(solution)/shard_map/pallas_call | solution.py:308
  95.2 0.0 collective-permute-done.3.refs_1_
  95.2 1.5 %collective-permute-done.4.refs_2_ = f32[1,1024]{1,0:T(1,128)S(1)} collective-permute-done((f32[1,1024]{1,0:T(1,128)S(1)}, f32[1,1024]{1,0:T(1,128)S(1)}, u32[]{:S(2)}, u32[]{:S(2)}) %collective-permute-start.4) | collective-permute-done | bytes 4128 | tf_op jit(solution)/shard_map/ppermute | solution.py:329
  96.6 5.4 %collective-permute-done.5.refs_3_ = f32[1,1024]{1,0:T(1,128)S(1)} collective-permute-done((f32[1,1024]{1,0:T(1,128)S(1)}, f32[1,1024]{1,0:T(1,128)S(1)}, u32[]{:S(2)}, u32[]{:S(2)}) %collective-permute-start.5) | collective-permute-done | bytes 4128 | tf_op jit(solution)/shard_map/ppermute | solution.py:329
  102.1 1.3 %shard_map.51 = f32[1,1024]{1,0:T(1,128)} custom-call(s32[1,1024]{1,0:T(1,128)S(1)} %get-tuple-element.13.land_ref, f32[1,1024]{1,0:T(1,128)S(1)} %shard_map.50.refs_0_, f32[1,1024]{1,0:T(1,128)S(1)} %collective-permute-done.3.refs_1_, f32[1,1024]{1,0:T(1,128)S(1)} %collective-permute-done.4.refs_2_, f32[1,1024]{1,0:T(1,128)S(1)} %collective-permute-done.5.refs_3_), custom_call_target="tpu_custom_call" | custom-call | flops 6442450944 | bytes 37748736 | tf_op jit(solution)/shard_map/pallas_call | solution.py:308
  (2 shorter events, 0.0 us)
Async XLA Ops:
  5.3 10.4 %copy-start = (s32[1024]{0:T(1024)S(1)}, s32[1024]{0:T(1024)}, u32[]{:S(2)}) copy-start(s32[1024]{0:T(1024)} %param.6) | copy-start | bytes 12292
  5.3 20.8 %copy-start.1 = (s32[1,4]{1,0:T(1,128)S(1)}, s32[1,4]{1,0:T(1,128)}, u32[]{:S(2)}) copy-start(s32[1,4]{1,0:T(1,128)} %param.7) | copy-start | bytes 52
  5.3 68.3 %all-to-all-start = ((bf16[64,296,128]{2,1,0:T(8,128)(2,1)}), bf16[64,296,128]{2,1,0:T(8,128)(2,1)}, u32[]{:S(2)}, u32[]{:S(2)}) async-start(bf16[64,296,128]{2,1,0:T(8,128)(2,1)} %shard_map.46), calls=%async_computation | async-start | bytes 9699328 | tf_op jit(solution)/shard_map/all_to_all | solution.py:347
  15.6 54.1 %collective-permute-start.1 = (s32[1,1024]{1,0:T(1,128)S(1)}, s32[1,1024]{1,0:T(1,128)S(1)}, u32[]{:S(2)}, u32[]{:S(2)}) collective-permute-start(s32[1,1024]{1,0:T(1,128)S(1)} %bitcast.4), channel_id=1, source_target_pairs={{4,0},{5,1},{6,2},{7,3},{8,4},{9,5},{10,6},{11,7},{12,8},{13,9},{1... | collective-permute-start | bytes 12296 | tf_op jit(solution)/shard_map/ppermute | solution.py:329
  22.9 46.8 %collective-permute-start = (s32[1,1024]{1,0:T(1,128)S(1)}, s32[1,1024]{1,0:T(1,128)S(1)}, u32[]{:S(2)}, u32[]{:S(2)}) collective-permute-start(s32[1,1024]{1,0:T(1,128)S(1)} %bitcast.5), channel_id=1, source_target_pairs={{2,0},{3,1},{4,2},{5,3},{6,4},{7,5},{8,6},{9,7},{10,8},{11,9},{12,... | collective-permute-start | bytes 12296 | tf_op jit(solution)/shard_map/ppermute | solution.py:329
  76.3 5.1 %collective-permute-start.2 = (bf16[1040,768]{1,0:T(8,128)(2,1)S(1)}, bf16[1040,768]{1,0:T(8,128)(2,1)S(1)}, u32[]{:S(2)}, u32[]{:S(2)}) collective-permute-start(bf16[1040,768]{1,0:T(8,128)(2,1)S(1)} %get-tuple-element.14.own_ref), channel_id=1, source_target_pairs={{0,1},{1,0},{2,3},{3,2},{4,5},{5,4},{6,7},{7,6},{8,9},{9,8},{10,11... | collective-permute-start | bytes 4792328 | tf_op jit(solution)/shard_map/ppermute | solution.py:329
  84.1 11.0 %collective-permute-start.3 = (f32[1,1024]{1,0:T(1,128)S(1)}, f32[1,1024]{1,0:T(1,128)S(1)}, u32[]{:S(2)}, u32[]{:S(2)}) collective-permute-start(f32[1,1024]{1,0:T(1,128)S(1)} %get-tuple-element.18), channel_id=1, source_target_pairs={{0,1},{1,0},{2,3},{3,2},{4,5},{5,4},{6,7},{7,6},{8,9},{9,8},{10,11... | collective-permute-start | bytes 12296 | tf_op jit(solution)/shard_map/ppermute | solution.py:329
  86.6 10.0 %collective-permute-start.4 = (f32[1,1024]{1,0:T(1,128)S(1)}, f32[1,1024]{1,0:T(1,128)S(1)}, u32[]{:S(2)}, u32[]{:S(2)}) collective-permute-start(f32[1,1024]{1,0:T(1,128)S(1)} %get-tuple-element.19), channel_id=1, source_target_pairs={{0,2},{1,3},{2,4},{3,5},{4,6},{5,7},{6,8},{7,9},{8,10},{9,11},{10,... | collective-permute-start | bytes 12296 | tf_op jit(solution)/shard_map/ppermute | solution.py:329
  91.8 10.3 %collective-permute-start.5 = (f32[1,1024]{1,0:T(1,128)S(1)}, f32[1,1024]{1,0:T(1,128)S(1)}, u32[]{:S(2)}, u32[]{:S(2)}) collective-permute-start(f32[1,1024]{1,0:T(1,128)S(1)} %get-tuple-element.20), channel_id=1, source_target_pairs={{0,4},{1,5},{2,6},{3,7},{4,8},{5,9},{6,10},{7,11},{8,12},{9,13},{1... | collective-permute-start | bytes 12296 | tf_op jit(solution)/shard_map/ppermute | solution.py:329

commit v2 on v1

--- a/solution.py
+++ b/solution.py
@@ -22,6 +22,8 @@
 MESSAGE = COPIES * BODY + HALF
 TAIL = 16
 DIGITS = 32
+CLUSTERS = 32
+STARTS_AT = 8
 AXES = ("gr", "gc")
 
 sharpness = 20.0
@@ -51,11 +53,13 @@
     return jnp.transpose(jnp.broadcast_to(row, (LANES, row.shape[1])))
 
 
-def front_kernel(devices, slot_hbm, emb_ref, out_hbm, slot_ref, raw_ref, unit_ref, digit_ref, info_ref, rows_ref, sems):
+def front_kernel(devices, slot_hbm, ids_hbm, emb_ref, out_hbm, slot_ref, ids_ref, raw_ref, unit_ref, digit_ref, info_ref, rows_ref, sems):
     size = 256
     parts = [pl.ds(at, size) for at in range(0, ROWS, size)]
     slots = pltpu.make_async_copy(slot_hbm, slot_ref, sems.at[len(parts)])
     slots.start()
+    ids = pltpu.make_async_copy(ids_hbm, ids_ref, sems.at[len(parts) + 1])
+    ids.start()
     copies = []
     for n, part in enumerate(parts):
         copies.append(pltpu.make_async_copy(emb_ref.at[part, :], raw_ref.at[part, :], sems.at[n]))
@@ -79,6 +83,9 @@
     even = iota((ROWS, LANES), 1) % 2 == 0
     digits = jnp.where(even, as_column(high.astype(F32)), as_column((low - high * DIGITS).astype(F32)))
     unit_ref[:, WIDTH:] = digits.astype(BF16)
+    ids.wait()
+    below = jnp.where(ids_ref[...] < iota((CLUSTERS, ROWS), 0), 1.0, 0.0)
+    starts = jnp.sum(below, axis=1, keepdims=True).astype(jnp.int32)
     for n, part in enumerate(parts):
         copies[n].wait()
         values = raw_ref[part, :].astype(F32)
@@ -89,7 +96,7 @@
     back = []
 
     def send(source, target):
-        back.append(pltpu.make_async_copy(source, target, sems.at[len(parts) + 1 + len(back)]))
+        back.append(pltpu.make_async_copy(source, target, sems.at[len(parts) + 2 + len(back)]))
         back[-1].start()
 
     lane = iota((per_part, HALF, LANES), 2)
@@ -117,6 +124,15 @@
         ahead = APART * copy
         far = jnp.concatenate([digit_ref[ahead:], digit_ref[:ahead]], axis=0)
         info = jnp.where(which == copy, far, info)
+    own_lane = iota((HALF, LANES), 1)
+    ahead = own_lane < 0
+    mine = jnp.zeros((HALF, LANES), jnp.int32)
+    for group in range(CLUSTERS // HALF):
+        value = starts[group * HALF:(group + 1) * HALF, :]
+        at = STARTS_AT + 2 * group
+        mine = jnp.where(own_lane == at, value // DIGITS, jnp.where(own_lane == at + 1, value % DIGITS, mine))
+        ahead = ahead | (own_lane == at) | (own_lane == at + 1)
+    info = jnp.where(ahead[None], mine.astype(F32)[None], info)
     info_ref[...] = info.astype(BF16)
     send(info_ref, out_hbm.at[:, pl.ds(COPIES * BODY, HALF), :])
     for copy in back:
@@ -147,26 +163,34 @@
     return [(digits[2 * c:2 * c + 1, :] * DIGITS + digits[2 * c + 1:2 * c + 2, :]).astype(jnp.int32) for c in copies]
 
 
-def arrival_ids(ids, land):
-    ids = jnp.broadcast_to(ids.astype(F32), (8, ROWS)).astype(BF16)
-    arrived = jnp.zeros((8, ROWS), F32)
-    for at in range(0, ROWS, 256):
-        place = one_hot(256, at, land)
-        arrived = arrived + jnp.dot(ids[:, at:at + 256], place, preferred_element_type=F32)
-    return arrived[0:1, :]
-
-
-def split_kernel(got_hbm, list_ref, *refs):
-    ids_refs, (out_ref, blocks_ref, far_ref, land_ref, digit_ref, sems) = refs[:COPIES], refs[COPIES:]
+def arrival_ids(tile, land):
+    tile = tile.astype(F32)
+    lane = iota((HALF, LANES), 1)
+    count = jnp.zeros((HALF, ROWS), F32)
+    for group in range(CLUSTERS // HALF):
+        at = STARTS_AT + 2 * group
+        digits = jnp.where(lane == at, tile * DIGITS, jnp.where(lane == at + 1, tile, 0.0))
+        starts = jnp.sum(digits, axis=1, keepdims=True).astype(jnp.int32)
+        count = count + jnp.where(starts <= land, 1.0, 0.0)
+    return jnp.sum(count, axis=0, keepdims=True) - 1.0
+
+
+def split_kernel(devices, position_ref, list_ref, got_hbm, out_ref, blocks_ref, ids_ref, land_ref, digit_ref, sems):
     slots = slot_tiles(got_hbm, digit_ref, sems.at[0, PIECES])
     rows = [tiles(got_hbm, c, blocks_ref.at[c], sems.at[c]) for c in range(COPIES)]
+    position = position_ref[0]
+    lane = iota((TAIL, LANES), 1)
+    entries = jnp.zeros((TAIL, LANES), F32)
+    for shift in range(1, SHIFTS + 1):
+        entry = jnp.where(position + shift < devices, list_ref[0, shift - 1], 0).astype(F32)
+        entries = jnp.where(lane == shift - 1, entry, entries)
     slots.wait()
     lands = arrival_slots(digit_ref[...], range(COPIES))
     land_ref[...] = lands[0]
     for c in range(COPIES):
-        far_ref[c] = arrival_ids(ids_refs[c][...], lands[c])
-    ids = far_ref[0]
-    entries = list_ref[...].astype(F32)
+        source = jnp.minimum(position + APART * c, devices - 1)
+        ids_ref[c] = arrival_ids(digit_ref[source], lands[c])
+    ids = ids_ref[0]
     row = iota((TAIL, LANES), 0)
     for at in range(0, WIDTH, LANES):
         rest = ids[:, at + WIDTH:at + WIDTH + LANES] if at + WIDTH < ROWS else jnp.zeros((1, LANES), F32)
@@ -267,13 +291,13 @@
     return part
 
 
-def second_kernel(core_ref, blocks_ref, ids_ref, sums_ref, sw_ref, *refs):
+def second_kernel(position_ref, blocks_ref, ids_ref, sums_ref, sw_ref, *refs):
     outs, (total, col, row_acc, col_acc) = refs[:COPIES + 1], refs[COPIES + 1:]
     total[...] = sums_ref[...]
     col[...] = as_column(ids_row(sw_ref))
     row_acc[...] = jnp.zeros_like(row_acc)
     for n in range(2):
-        which = 1 - core_ref[0] + n
+        which = 1 - position_ref[0] % 2 + n
         pair(
             sw_ref, col, block_part(blocks_ref, which), ids_ref[which], weight_of(sw_ref, 1 + 2 * n), row_acc,
             col_acc, total.at[which],
@@ -331,35 +355,30 @@
 
 def local(embeddings, sorted_slot, cluster_ids, block_list):
     devices = lax.axis_size(AXES)
-    position = lax.axis_index(AXES)
-    core = (position % 2).astype(jnp.int32).reshape(1)
+    position = lax.axis_index(AXES).astype(jnp.int32).reshape(1)
     move_d = functools.partial(move, devices=devices)
     scratch = pltpu.VMEM
 
     outgoing = call(
         functools.partial(front_kernel, devices),
-        jax.ShapeDtypeStruct((devices, MESSAGE, LANES), BF16), [ANY] * 2,
-        [scratch((1, ROWS), jnp.int32), scratch((ROWS, WIDTH), BF16), scratch((ROWS, WIDTH + LANES), BF16)]
+        jax.ShapeDtypeStruct((devices, MESSAGE, LANES), BF16), [ANY] * 3,
+        [scratch((1, ROWS), jnp.int32)] * 2 + [scratch((ROWS, WIDTH), BF16), scratch((ROWS, WIDTH + LANES), BF16)]
         + [scratch((devices, HALF, LANES), F32), scratch((devices, HALF, LANES), BF16)]
         + [scratch((devices, BODY, LANES), BF16), pltpu.SemaphoreType.DMA((24,))],
-        1, (sorted_slot.reshape(1, ROWS), embeddings), 62, ANY,
+        1, (sorted_slot.reshape(1, ROWS), cluster_ids.reshape(1, ROWS), embeddings), 62, ANY,
     )
     got = lax.all_to_all(outgoing, AXES, split_axis=0, concat_axis=0, tiled=True)
-    ids = cluster_ids.reshape(1, ROWS)
-    far_ids = [move_d(ids, change=lambda p, c=c: p - APART * c) for c in range(1, COPIES)]
-    reach = position + 1 + jnp.arange(SHIFTS, dtype=jnp.int32)
-    entries = jnp.pad(jnp.where(reach[None, :] < devices, block_list, 0), ((0, 0), (0, LANES - SHIFTS)))
     sems = pltpu.SemaphoreType.DMA
     own, blocks, block_ids, land = call(
-        split_kernel,
+        functools.partial(split_kernel, devices),
         [
             jax.ShapeDtypeStruct((ROWS + TAIL, WIDTH), BF16),
             jax.ShapeDtypeStruct((COPIES, devices, PER_PAIR, WIDTH), BF16),
             jax.ShapeDtypeStruct((COPIES, 1, ROWS), F32),
             jax.ShapeDtypeStruct((1, ROWS), jnp.int32),
         ],
-        [ANY] + [VMEM] * (1 + COPIES), [scratch((devices, HALF, LANES), BF16), sems((COPIES, PIECES + 1))],
-        0.5, (got, entries, ids, *far_ids), 16,
+        [SMEM, SMEM, ANY], [scratch((devices, HALF, LANES), BF16), sems((COPIES, PIECES + 1))],
+        0.5, (position, block_list, got), 16,
     )
     sw = move_d(own, change=lambda p: p ^ 1)
     sides = [scratch((ROWS, LANES), F32)] * 2 + [scratch((8, ROWS), F32)]
@@ -369,7 +388,7 @@
     sums = call(
         second_kernel, [vec(ROWS)] * (COPIES + 1), [SMEM] + [VMEM] * 4,
         [scratch((COPIES, 1, ROWS), F32)] + sides,
-        2, (core, blocks, block_ids, sums, sw), 16,
+        2, (position, blocks, block_ids, sums, sw), 16,
     )
     own_sum = call(
         self_kernel, vec(ROWS), [VMEM] * 2, sides,

time: 104 us -> 103 us (level)
  the two profiles are of different devices: /device:TPU:34 before, /device:TPU:32 now
where the time goes in v2:
time: 103 us; the launch traced here: 101 us
  waiting for transfers between devices  67.1 us (65%)
  starting transfers between devices  17.1 us (17%)
  Pallas kernels  16.8 us (16%)
    all_to_all x1, waiting for transfers between devices, local(): lax.all_to_all(outgoing, AXES, split_axis=0, concat_axis=0, tiled=True)  57.8 us
    pallas_call x6, Pallas kernels, call(): pl.pallas_call(kernel, out_shape=out_shape, in_specs=in_specs, out_specs=...  16.8 us
    all_to_all x1, starting transfers between devices, local(): lax.all_to_all(outgoing, AXES, split_axis=0, concat_axis=0, tiled=True)  11.3 us
    ppermute x4, waiting for transfers between devices, move(): return lax.ppermute(value, AXES, pairs)  9.29 us
    ppermute x4, starting transfers between devices, move(): return lax.ppermute(value, AXES, pairs)  5.8 us
  transfers between devices with their start and end apart: 5, of which 4 were waited for; matrix products, arithmetic and copies ran while one was open for 0% of the time, Pallas kernels for 2%

profile of v2, /device:TPU:32, one launch (start us, length us, event | category | flops | bytes accessed | tf_op | source)
XLA Modules:
  0.0 101.1 jit_solution(9031146294560726389)
XLA Ops:
  0.0 5.3 %shard_map.46 = bf16[64,296,128]{2,1,0:T(8,128)(2,1)} custom-call(s32[1,1024]{1,0:T(1,128)} %bitcast.4, s32[1,1024]{1,0:T(1,128)} %bitcast.5, bf16[1024,768]{1,0:T(8,128)(2,1)} %emb_ref.1), custom_call_target="tpu_custom_call" | custom-call | flops 32212254720 | bytes 62914560 | tf_op jit(solution)/shard_map/pallas_call | solution.py:332
  5.3 0.0 copy-start
  5.3 11.3 %all-to-all-start = ((bf16[64,296,128]{2,1,0:T(8,128)(2,1)}), bf16[64,296,128]{2,1,0:T(8,128)(2,1)}, u32[]{:S(2)}, u32[]{:S(2)}) async-start(bf16[64,296,128]{2,1,0:T(8,128)(2,1)} %shard_map.46), calls=%async_computation | async-start | bytes 9699328 | tf_op jit(solution)/shard_map/all_to_all | solution.py:370
  16.6 57.8 %all-to-all-done.got_hbm = bf16[64,296,128]{2,1,0:T(8,128)(2,1)} async-done(((bf16[64,296,128]{2,1,0:T(8,128)(2,1)}), bf16[64,296,128]{2,1,0:T(8,128)(2,1)}, u32[]{:S(2)}, u32[]{:S(2)}) %all-to-all-start) | async-done | bytes 4849696 | tf_op jit(solution)/shard_map/all_to_all | solution.py:370
  74.4 0.0 copy-done
  74.4 3.2 %shard_map.47 = (bf16[1040,768]{1,0:T(8,128)(2,1)S(1)}, bf16[3,64,16,768]{3,2,1,0:T(8,128)(2,1)S(1)}, f32[3,1,1024]{2,1,0:T(1,128)S(1)}, s32[1,1024]{1,0:T(1,128)S(1)}) custom-call(s32[1]{0:T(128)} %bitcast.position_ref, s32[1,4]{1,0:T(1,128)S(1)} %copy-done, bf16[64,296,128]{2,1,0:T(8,128)(2,1)} %all-to-all-done.got_hbm), custom_call_target="tpu_custom_call" | custom-call | flops 16106127360 | bytes 47185920 | tf_op jit(solution)/shard_map/pallas_call | solution.py:332
  77.6 0.5 collective-permute-start
  78.1 0.6 shard_map.48.sums_ref
  78.7 2.5 %collective-permute-done.sw_ref = bf16[1040,768]{1,0:T(8,128)(2,1)S(1)} collective-permute-done((bf16[1040,768]{1,0:T(8,128)(2,1)S(1)}, bf16[1040,768]{1,0:T(8,128)(2,1)S(1)}, u32[]{:S(2)}, u32[]{:S(2)}) %collective-permute-start) | collective-permute-done | bytes 1597472 | tf_op jit(solution)/shard_map/ppermute | solution.py:353
  81.2 5.1 %shard_map.49 = (f32[1,1024]{1,0:T(1,128)S(1)}, f32[1,1024]{1,0:T(1,128)S(1)}, f32[1,1024]{1,0:T(1,128)S(1)}, f32[1,1024]{1,0:T(1,128)S(1)}) custom-call(s32[1]{0:T(128)} %bitcast.position_ref, bf16[3,64,16,768]{3,2,1,0:T(8,128)(2,1)S(1)} %get-tuple-element.15.blocks_ref, f32[3,1,1024]{2,1,0:T(1,128)S(1)} %get-tuple-element.16.ids_ref, ...), custom_call_target="tpu_custom_call" | custom-call | flops 64424509440 | bytes 94371840 | tf_op jit(solution)/shard_map/pallas_call | solution.py:332
  86.3 0.1 collective-permute-start.1
  86.4 3.1 %collective-permute-start.2 = (f32[1,1024]{1,0:T(1,128)S(1)}, f32[1,1024]{1,0:T(1,128)S(1)}, u32[]{:S(2)}, u32[]{:S(2)}) collective-permute-start(f32[1,1024]{1,0:T(1,128)S(1)} %get-tuple-element.19), channel_id=1, source_target_pairs={{0,2},{1,3},{2,4},{3,5},{4,6},{5,7},{6,8},{7,9},{8,10},{9,11},{10,... | collective-permute-start | bytes 12296 | tf_op jit(solution)/shard_map/ppermute | solution.py:353
  89.5 2.1 %collective-permute-start.3 = (f32[1,1024]{1,0:T(1,128)S(1)}, f32[1,1024]{1,0:T(1,128)S(1)}, u32[]{:S(2)}, u32[]{:S(2)}) collective-permute-start(f32[1,1024]{1,0:T(1,128)S(1)} %get-tuple-element.20), channel_id=1, source_target_pairs={{0,4},{1,5},{2,6},{3,7},{4,8},{5,9},{6,10},{7,11},{8,12},{9,13},{1... | collective-permute-start | bytes 12296 | tf_op jit(solution)/shard_map/ppermute | solution.py:353
  91.6 1.4 %shard_map.50.refs_0_ = f32[1,1024]{1,0:T(1,128)S(1)} custom-call(bf16[1040,768]{1,0:T(8,128)(2,1)S(1)} %get-tuple-element.14.own_ref, f32[1,1024]{1,0:T(1,128)S(1)} %get-tuple-element.17.sum_ref), custom_call_target="tpu_custom_call" | custom-call | flops 19327352832 | bytes 50331648 | tf_op jit(solution)/shard_map/pallas_call | solution.py:332
  93.0 0.0 collective-permute-done.1.refs_1_
  93.0 3.4 %collective-permute-done.2.refs_2_ = f32[1,1024]{1,0:T(1,128)S(1)} collective-permute-done((f32[1,1024]{1,0:T(1,128)S(1)}, f32[1,1024]{1,0:T(1,128)S(1)}, u32[]{:S(2)}, u32[]{:S(2)}) %collective-permute-start.2) | collective-permute-done | bytes 4128 | tf_op jit(solution)/shard_map/ppermute | solution.py:353
  96.4 3.4 %collective-permute-done.3.refs_3_ = f32[1,1024]{1,0:T(1,128)S(1)} collective-permute-done((f32[1,1024]{1,0:T(1,128)S(1)}, f32[1,1024]{1,0:T(1,128)S(1)}, u32[]{:S(2)}, u32[]{:S(2)}) %collective-permute-start.3) | collective-permute-done | bytes 4128 | tf_op jit(solution)/shard_map/ppermute | solution.py:353
  99.8 1.3 %shard_map.51 = f32[1,1024]{1,0:T(1,128)} custom-call(s32[1,1024]{1,0:T(1,128)S(1)} %get-tuple-element.13.land_ref, f32[1,1024]{1,0:T(1,128)S(1)} %shard_map.50.refs_0_, f32[1,1024]{1,0:T(1,128)S(1)} %collective-permute-done.1.refs_1_, f32[1,1024]{1,0:T(1,128)S(1)} %collective-permute-done.2.refs_2_, f32[1,1024]{1,0:T(1,128)S(1)} %collective-permute-done.3.refs_3_), custom_call_target="tpu_custom_call" | custom-call | flops 6442450944 | bytes 37748736 | tf_op jit(solution)/shard_map/pallas_call | solution.py:332
Async XLA Ops:
  5.3 69.1 %copy-start = (s32[1,4]{1,0:T(1,128)S(1)}, s32[1,4]{1,0:T(1,128)}, u32[]{:S(2)}) copy-start(s32[1,4]{1,0:T(1,128)} %list_ref.1) | copy-start | bytes 52
  5.3 69.1 %all-to-all-start = ((bf16[64,296,128]{2,1,0:T(8,128)(2,1)}), bf16[64,296,128]{2,1,0:T(8,128)(2,1)}, u32[]{:S(2)}, u32[]{:S(2)}) async-start(bf16[64,296,128]{2,1,0:T(8,128)(2,1)} %shard_map.46), calls=%async_computation | async-start | bytes 9699328 | tf_op jit(solution)/shard_map/all_to_all | solution.py:370
  77.6 3.6 %collective-permute-start = (bf16[1040,768]{1,0:T(8,128)(2,1)S(1)}, bf16[1040,768]{1,0:T(8,128)(2,1)S(1)}, u32[]{:S(2)}, u32[]{:S(2)}) collective-permute-start(bf16[1040,768]{1,0:T(8,128)(2,1)S(1)} %get-tuple-element.14.own_ref), channel_id=1, source_target_pairs={{0,1},{1,0},{2,3},{3,2},{4,5},{5,4},{6,7},{7,6},{8,9},{9,8},{10,11... | collective-permute-start | bytes 4792328 | tf_op jit(solution)/shard_map/ppermute | solution.py:353
  86.3 6.7 %collective-permute-start.1 = (f32[1,1024]{1,0:T(1,128)S(1)}, f32[1,1024]{1,0:T(1,128)S(1)}, u32[]{:S(2)}, u32[]{:S(2)}) collective-permute-start(f32[1,1024]{1,0:T(1,128)S(1)} %get-tuple-element.18), channel_id=1, source_target_pairs={{0,1},{1,0},{2,3},{3,2},{4,5},{5,4},{6,7},{7,6},{8,9},{9,8},{10,11... | collective-permute-start | bytes 12296 | tf_op jit(solution)/shard_map/ppermute | solution.py:353
  86.4 10.0 %collective-permute-start.2 = (f32[1,1024]{1,0:T(1,128)S(1)}, f32[1,1024]{1,0:T(1,128)S(1)}, u32[]{:S(2)}, u32[]{:S(2)}) collective-permute-start(f32[1,1024]{1,0:T(1,128)S(1)} %get-tuple-element.19), channel_id=1, source_target_pairs={{0,2},{1,3},{2,4},{3,5},{4,6},{5,7},{6,8},{7,9},{8,10},{9,11},{10,... | collective-permute-start | bytes 12296 | tf_op jit(solution)/shard_map/ppermute | solution.py:353
  89.5 10.3 %collective-permute-start.3 = (f32[1,1024]{1,0:T(1,128)S(1)}, f32[1,1024]{1,0:T(1,128)S(1)}, u32[]{:S(2)}, u32[]{:S(2)}) collective-permute-start(f32[1,1024]{1,0:T(1,128)S(1)} %get-tuple-element.20), channel_id=1, source_target_pairs={{0,4},{1,5},{2,6},{3,7},{4,8},{5,9},{6,10},{7,11},{8,12},{9,13},{1... | collective-permute-start | bytes 12296 | tf_op jit(solution)/shard_map/ppermute | solution.py:353

commit v3 on v1

--- a/solution.py
+++ b/solution.py
@@ -159,7 +159,7 @@
 def split_kernel(got_hbm, list_ref, *refs):
     ids_refs, (out_ref, blocks_ref, far_ref, land_ref, digit_ref, sems) = refs[:COPIES], refs[COPIES:]
     slots = slot_tiles(got_hbm, digit_ref, sems.at[0, PIECES])
-    rows = [tiles(got_hbm, c, blocks_ref.at[c], sems.at[c]) for c in range(COPIES)]
+    rows = [tiles(got_hbm, c, blocks_ref.at[c], sems.at[c]) for c in range(COPIES - 1)]
     slots.wait()
     lands = arrival_slots(digit_ref[...], range(COPIES))
     land_ref[...] = lands[0]
@@ -175,7 +175,7 @@
     for copy in rows[0]:
         copy.wait()
     out_ref[0:ROWS, :] = blocks_ref[0].reshape(ROWS, WIDTH)
-    for copy in (*rows[1], *rows[2]):
+    for copy in rows[1]:
         copy.wait()
 
 
@@ -238,19 +238,22 @@
     return jnp.sum(jnp.transpose(acc[...]), axis=0, keepdims=True)
 
 
-def first_kernel(own_ref, blocks_ref, ids_ref, sums_ref, col, row_acc, col_acc):
+def first_kernel(got_hbm, own_ref, near_ref, ids_ref, sums_ref, far_ref, col, row_acc, col_acc, sems):
+    rows = [tiles(got_hbm, c, far_ref.at[c - 1], sems.at[c]) for c in range(COPIES - 1, 0, -1)]
     col[...] = as_column(ids_ref[0])
     row_acc[...] = jnp.zeros_like(row_acc)
     sums_ref[...] = jnp.zeros_like(sums_ref)
     for c in range(1, COPIES):
-        pair(
-            own_ref, col, block_part(blocks_ref, c), ids_ref[c], weight_of(own_ref, APART * c), row_acc, col_acc,
-            sums_ref.at[c],
-        )
+        block = block_part(near_ref, 1) if c == 1 else block_part(far_ref, 1)
+        pair(own_ref, col, block, ids_ref[c], weight_of(own_ref, APART * c), row_acc, col_acc, sums_ref.at[c])
+        for copy in rows.pop(0):
+            copy.wait()
     sums_ref[0] = fold_rows(row_acc)
 
 
-def self_kernel(own_ref, sum_ref, out_ref, col, row_acc, col_acc):
+def self_kernel(own_ref, land_ref, sum_ref, out_ref, place_ref, col, row_acc, col_acc):
+    for at in range(0, ROWS, 256):
+        place_ref[at:at + 256, :] = one_hot(256, at, land_ref[...])
     row = ids_row(own_ref)
     col[...] = as_column(row)
     row_acc[...] = jnp.zeros_like(row_acc)
@@ -267,7 +270,7 @@
     return part
 
 
-def second_kernel(core_ref, blocks_ref, ids_ref, sums_ref, sw_ref, *refs):
+def second_kernel(core_ref, near_ref, far_ref, ids_ref, sums_ref, sw_ref, *refs):
     outs, (total, col, row_acc, col_acc) = refs[:COPIES + 1], refs[COPIES + 1:]
     total[...] = sums_ref[...]
     col[...] = as_column(ids_row(sw_ref))
@@ -275,7 +278,7 @@
     for n in range(2):
         which = 1 - core_ref[0] + n
         pair(
-            sw_ref, col, block_part(blocks_ref, which), ids_ref[which], weight_of(sw_ref, 1 + 2 * n), row_acc,
+            sw_ref, col, block_part(far_ref if n else near_ref, 1 - core_ref[0]), ids_ref[which], weight_of(sw_ref, 1 + 2 * n), row_acc,
             col_acc, total.at[which],
         )
     for c in range(COPIES):
@@ -283,7 +286,7 @@
     outs[COPIES][...] = fold_rows(row_acc)
 
 
-def end_kernel(land_ref, *refs):
+def end_kernel(place_ref, *refs):
     out_ref = refs[-1]
     load = refs[0][...]
     for ref in refs[1:-1]:
@@ -295,7 +298,7 @@
     which = iota((8, ROWS), 0)
     parts = jnp.where(which == 0, high, jnp.where(which == 1, mid, jnp.where(which == 2, low, 0.0))).astype(BF16)
     for step in range(4):
-        placed = nt(parts, one_hot(256, step * 256, land_ref[...]))
+        placed = nt(parts, place_ref[step * 256:(step + 1) * 256, :])
         out_ref[:, step * 256:(step + 1) * 256] = placed[0:1, :] + placed[1:2, :] + placed[2:3, :]
 
 
@@ -350,11 +353,12 @@
     reach = position + 1 + jnp.arange(SHIFTS, dtype=jnp.int32)
     entries = jnp.pad(jnp.where(reach[None, :] < devices, block_list, 0), ((0, 0), (0, LANES - SHIFTS)))
     sems = pltpu.SemaphoreType.DMA
-    own, blocks, block_ids, land = call(
+    two_blocks = jax.ShapeDtypeStruct((2, devices, PER_PAIR, WIDTH), BF16)
+    own, near, block_ids, land = call(
         split_kernel,
         [
             jax.ShapeDtypeStruct((ROWS + TAIL, WIDTH), BF16),
-            jax.ShapeDtypeStruct((COPIES, devices, PER_PAIR, WIDTH), BF16),
+            two_blocks,
             jax.ShapeDtypeStruct((COPIES, 1, ROWS), F32),
             jax.ShapeDtypeStruct((1, ROWS), jnp.int32),
         ],
@@ -363,21 +367,22 @@
     )
     sw = move_d(own, change=lambda p: p ^ 1)
     sides = [scratch((ROWS, LANES), F32)] * 2 + [scratch((8, ROWS), F32)]
+    sums, far = call(
+        first_kernel, [jax.ShapeDtypeStruct((COPIES, 1, ROWS), F32), two_blocks], [ANY] + [VMEM] * 3,
+        sides + [sems((COPIES, PIECES))], 2, (got, own, near, block_ids), 16,
+    )
     sums = call(
-        first_kernel, jax.ShapeDtypeStruct((COPIES, 1, ROWS), F32), [VMEM] * 3, sides, 2, (own, blocks, block_ids), 16
-    )
-    sums = call(
-        second_kernel, [vec(ROWS)] * (COPIES + 1), [SMEM] + [VMEM] * 4,
+        second_kernel, [vec(ROWS)] * (COPIES + 1), [SMEM] + [VMEM] * 5,
         [scratch((COPIES, 1, ROWS), F32)] + sides,
-        2, (core, blocks, block_ids, sums, sw), 16,
-    )
-    own_sum = call(
-        self_kernel, vec(ROWS), [VMEM] * 2, sides,
-        0.6, (own, sums[0]), 16,
+        2, (core, near, far, block_ids, sums, sw), 16,
+    )
+    own_sum, place = call(
+        self_kernel, [vec(ROWS), jax.ShapeDtypeStruct((ROWS, ROWS), BF16)], [VMEM] * 3, sides,
+        0.6, (own, land, sums[0]), 16,
     )
     returned = [own_sum, move_d(sums[COPIES], change=lambda p: p ^ 1)]
     returned += [move_d(sums[c], change=lambda p, c=c: p + APART * c) for c in range(1, COPIES)]
-    weights = call(end_kernel, vec(ROWS), [VMEM] * (COPIES + 2), [], 0.2, (land, *returned))
+    weights = call(end_kernel, vec(ROWS), [VMEM] * (COPIES + 2), [], 0.2, (place, *returned))
     return weights.reshape(ROWS)
 
 

time: 104 us -> 103 us (level)
  the two profiles are of different devices: /device:TPU:34 before, /device:TPU:24 now
where the time goes in v3:
time: 103 us; the launch traced here: 102 us
  waiting for transfers between devices  54.1 us (53%)
  starting transfers between devices  34.5 us (33%)
  Pallas kernels  13.6 us (13%)
    ppermute x6, waiting for transfers between devices, move(): return lax.ppermute(value, AXES, pairs)  54.1 us
    ppermute x6, starting transfers between devices, move(): return lax.ppermute(value, AXES, pairs)  23.2 us
    pallas_call x6, Pallas kernels, call(): pl.pallas_call(kernel, out_shape=out_shape, in_specs=in_specs, out_specs=...  13.6 us
    all_to_all x1, starting transfers between devices, local(): lax.all_to_all(outgoing, AXES, split_axis=0, concat_axis=0, tiled=True)  11.4 us
  transfers between devices with their start and end apart: 7, of which 4 were waited for; matrix products, arithmetic and copies ran while one was open for 0% of the time, Pallas kernels for 4%

profile of v3, /device:TPU:24, one launch (start us, length us, event | category | flops | bytes accessed | tf_op | source)
XLA Modules:
  0.0 102.4 jit_solution(4070674174850802188)
XLA Ops:
  0.0 5.2 %shard_map.46 = bf16[64,296,128]{2,1,0:T(8,128)(2,1)} custom-call(s32[1,1024]{1,0:T(1,128)} %bitcast.7, bf16[1024,768]{1,0:T(8,128)(2,1)} %emb_ref.1), custom_call_target="tpu_custom_call" | custom-call | flops 32212254720 | bytes 62914560 | tf_op jit(solution)/shard_map/pallas_call | solution.py:311
  5.2 0.0 copy-start
  5.3 0.0 copy-start.1
  5.3 11.4 %all-to-all-start = ((bf16[64,296,128]{2,1,0:T(8,128)(2,1)}), bf16[64,296,128]{2,1,0:T(8,128)(2,1)}, u32[]{:S(2)}, u32[]{:S(2)}) async-start(bf16[64,296,128]{2,1,0:T(8,128)(2,1)} %shard_map.46), calls=%async_computation | async-start | bytes 9699328 | tf_op jit(solution)/shard_map/all_to_all | solution.py:350
  16.6 0.0 copy-done
  16.6 2.8 %collective-permute-start = (s32[1,1024]{1,0:T(1,128)S(1)}, s32[1,1024]{1,0:T(1,128)S(1)}, u32[]{:S(2)}, u32[]{:S(2)}) collective-permute-start(s32[1,1024]{1,0:T(1,128)S(1)} %bitcast.4), channel_id=1, source_target_pairs={{2,0},{3,1},{4,2},{5,3},{6,4},{7,5},{8,6},{9,7},{10,8},{11,9},{12,... | collective-permute-start | bytes 12296 | tf_op jit(solution)/shard_map/ppermute | solution.py:332
  19.4 3.0 %collective-permute-start.1 = (s32[1,1024]{1,0:T(1,128)S(1)}, s32[1,1024]{1,0:T(1,128)S(1)}, u32[]{:S(2)}, u32[]{:S(2)}) collective-permute-start(s32[1,1024]{1,0:T(1,128)S(1)} %bitcast.5), channel_id=1, source_target_pairs={{4,0},{5,1},{6,2},{7,3},{8,4},{9,5},{10,6},{11,7},{12,8},{13,9},{1... | collective-permute-start | bytes 12296 | tf_op jit(solution)/shard_map/ppermute | solution.py:332
  22.5 0.0 copy-done.1
  22.5 50.0 %collective-permute-done.refs_1_ = s32[1,1024]{1,0:T(1,128)S(1)} collective-permute-done((s32[1,1024]{1,0:T(1,128)S(1)}, s32[1,1024]{1,0:T(1,128)S(1)}, u32[]{:S(2)}, u32[]{:S(2)}) %collective-permute-start) | collective-permute-done | bytes 4128 | tf_op jit(solution)/shard_map/ppermute | solution.py:332
  72.5 0.9 collective-permute-done.1.refs_2_
  73.4 0.0 all-to-all-done.got_hbm
  73.4 2.3 %shard_map.47 = (bf16[1040,768]{1,0:T(8,128)(2,1)S(1)}, bf16[2,64,16,768]{3,2,1,0:T(8,128)(2,1)S(1)}, f32[3,1,1024]{2,1,0:T(1,128)S(1)}, s32[1,1024]{1,0:T(1,128)S(1)}) custom-call(bf16[64,296,128]{2,1,0:T(8,128)(2,1)} %all-to-all-done.got_hbm, s32[1,128]{1,0:T(1,128)S(1)} %pad.4.list_ref, s32[1,1024]{1,0:T(1,128)S(1)} %bitcast.6, ...), custom_call_target="tpu_custom_call" | custom-call | flops 16106127360 | bytes 47185920 | tf_op jit(solution)/shard_map/pallas_call | solution.py:311
  75.7 0.1 collective-permute-start.2
  75.8 2.3 %shard_map.48 = (f32[3,1,1024]{2,1,0:T(1,128)S(1)}, bf16[2,64,16,768]{3,2,1,0:T(8,128)(2,1)S(1)}) custom-call(bf16[64,296,128]{2,1,0:T(8,128)(2,1)} %all-to-all-done.got_hbm, bf16[1040,768]{1,0:T(8,128)(2,1)S(1)} %get-tuple-element.17.own_ref, bf16[2,64,16,768]{3,2,1,0:T(8,128)(2,1)S(1)} %get-tuple-element.19.near_ref, ...), custom_call_target="tpu_custom_call" | custom-call | flops 64424509440 | bytes 94371840 | tf_op jit(solution)/shard_map/pallas_call | solution.py:311
  78.0 1.2 %collective-permute-done.2.sw_ref = bf16[1040,768]{1,0:T(8,128)(2,1)S(1)} collective-permute-done((bf16[1040,768]{1,0:T(8,128)(2,1)S(1)}, bf16[1040,768]{1,0:T(8,128)(2,1)S(1)}, u32[]{:S(2)}, u32[]{:S(2)}) %collective-permute-start.2) | collective-permute-done | bytes 1597472 | tf_op jit(solution)/shard_map/ppermute | solution.py:332
  79.2 0.8 shard_map.49
  80.0 2.4 %collective-permute-start.3 = (f32[1,1024]{1,0:T(1,128)S(1)}, f32[1,1024]{1,0:T(1,128)S(1)}, u32[]{:S(2)}, u32[]{:S(2)}) collective-permute-start(f32[1,1024]{1,0:T(1,128)S(1)} %get-tuple-element.26), channel_id=1, source_target_pairs={{0,1},{1,0},{2,3},{3,2},{4,5},{5,4},{6,7},{7,6},{8,9},{9,8},{10,11... | collective-permute-start | bytes 12296 | tf_op jit(solution)/shard_map/ppermute | solution.py:332
  82.4 11.8 %collective-permute-start.4 = (f32[1,1024]{1,0:T(1,128)S(1)}, f32[1,1024]{1,0:T(1,128)S(1)}, u32[]{:S(2)}, u32[]{:S(2)}) collective-permute-start(f32[1,1024]{1,0:T(1,128)S(1)} %get-tuple-element.27), channel_id=1, source_target_pairs={{0,2},{1,3},{2,4},{3,5},{4,6},{5,7},{6,8},{7,9},{8,10},{9,11},{10,... | collective-permute-start | bytes 12296 | tf_op jit(solution)/shard_map/ppermute | solution.py:332
  94.2 3.1 %collective-permute-start.5 = (f32[1,1024]{1,0:T(1,128)S(1)}, f32[1,1024]{1,0:T(1,128)S(1)}, u32[]{:S(2)}, u32[]{:S(2)}) collective-permute-start(f32[1,1024]{1,0:T(1,128)S(1)} %get-tuple-element.28), channel_id=1, source_target_pairs={{0,4},{1,5},{2,6},{3,7},{4,8},{5,9},{6,10},{7,11},{8,12},{9,13},{1... | collective-permute-start | bytes 12296 | tf_op jit(solution)/shard_map/ppermute | solution.py:332
  97.3 1.8 %shard_map.50 = (f32[1,1024]{1,0:T(1,128)S(1)}, bf16[1024,1024]{1,0:T(8,128)(2,1)S(1)}) custom-call(bf16[1040,768]{1,0:T(8,128)(2,1)S(1)} %get-tuple-element.17.own_ref, s32[1,1024]{1,0:T(1,128)S(1)} %get-tuple-element.18.land_ref, f32[1,1024]{1,0:T(1,128)S(1)} %get-tuple-element.23.sum_ref), custom_call_target="tpu_custom_call" | custom-call | flops 19327352832 | bytes 50331648 | tf_op jit(solution)/shard_map/pallas_call | solution.py:311
  99.1 0.0 collective-permute-done.3.refs_1_
  99.1 0.0 collective-permute-done.4.refs_2_
  99.1 2.0 %collective-permute-done.5.refs_3_ = f32[1,1024]{1,0:T(1,128)S(1)} collective-permute-done((f32[1,1024]{1,0:T(1,128)S(1)}, f32[1,1024]{1,0:T(1,128)S(1)}, u32[]{:S(2)}, u32[]{:S(2)}) %collective-permute-start.5) | collective-permute-done | bytes 4128 | tf_op jit(solution)/shard_map/ppermute | solution.py:332
  101.2 1.3 %shard_map.51 = f32[1,1024]{1,0:T(1,128)} custom-call(bf16[1024,1024]{1,0:T(8,128)(2,1)S(1)} %get-tuple-element.24.place_ref, f32[1,1024]{1,0:T(1,128)S(1)} %get-tuple-element.25.refs_0_, f32[1,1024]{1,0:T(1,128)S(1)} %collective-permute-done.3.refs_1_, f32[1,1024]{1,0:T(1,128)S(1)} %collective-permute-done.4.refs_2_, ...), custom_call_target="tpu_custom_call" | custom-call | flops 6442450944 | bytes 37748736 | tf_op jit(solution)/shard_map/pallas_call | solution.py:311
  (2 shorter events, 0.0 us)
Async XLA Ops:
  5.2 11.4 %copy-start = (s32[1024]{0:T(1024)S(1)}, s32[1024]{0:T(1024)}, u32[]{:S(2)}) copy-start(s32[1024]{0:T(1024)} %param.6) | copy-start | bytes 12292
  5.3 17.2 %copy-start.1 = (s32[1,4]{1,0:T(1,128)S(1)}, s32[1,4]{1,0:T(1,128)}, u32[]{:S(2)}) copy-start(s32[1,4]{1,0:T(1,128)} %param.7) | copy-start | bytes 52
  5.3 68.1 %all-to-all-start = ((bf16[64,296,128]{2,1,0:T(8,128)(2,1)}), bf16[64,296,128]{2,1,0:T(8,128)(2,1)}, u32[]{:S(2)}, u32[]{:S(2)}) async-start(bf16[64,296,128]{2,1,0:T(8,128)(2,1)} %shard_map.46), calls=%async_computation | async-start | bytes 9699328 | tf_op jit(solution)/shard_map/all_to_all | solution.py:350
  16.6 55.8 %collective-permute-start = (s32[1,1024]{1,0:T(1,128)S(1)}, s32[1,1024]{1,0:T(1,128)S(1)}, u32[]{:S(2)}, u32[]{:S(2)}) collective-permute-start(s32[1,1024]{1,0:T(1,128)S(1)} %bitcast.4), channel_id=1, source_target_pairs={{2,0},{3,1},{4,2},{5,3},{6,4},{7,5},{8,6},{9,7},{10,8},{11,9},{12,... | collective-permute-start | bytes 12296 | tf_op jit(solution)/shard_map/ppermute | solution.py:332
  19.4 54.0 %collective-permute-start.1 = (s32[1,1024]{1,0:T(1,128)S(1)}, s32[1,1024]{1,0:T(1,128)S(1)}, u32[]{:S(2)}, u32[]{:S(2)}) collective-permute-start(s32[1,1024]{1,0:T(1,128)S(1)} %bitcast.5), channel_id=1, source_target_pairs={{4,0},{5,1},{6,2},{7,3},{8,4},{9,5},{10,6},{11,7},{12,8},{13,9},{1... | collective-permute-start | bytes 12296 | tf_op jit(solution)/shard_map/ppermute | solution.py:332
  75.7 3.5 %collective-permute-start.2 = (bf16[1040,768]{1,0:T(8,128)(2,1)S(1)}, bf16[1040,768]{1,0:T(8,128)(2,1)S(1)}, u32[]{:S(2)}, u32[]{:S(2)}) collective-permute-start(bf16[1040,768]{1,0:T(8,128)(2,1)S(1)} %get-tuple-element.17.own_ref), channel_id=1, source_target_pairs={{0,1},{1,0},{2,3},{3,2},{4,5},{5,4},{6,7},{7,6},{8,9},{9,8},{10,11... | collective-permute-start | bytes 4792328 | tf_op jit(solution)/shard_map/ppermute | solution.py:332
  80.0 19.1 %collective-permute-start.3 = (f32[1,1024]{1,0:T(1,128)S(1)}, f32[1,1024]{1,0:T(1,128)S(1)}, u32[]{:S(2)}, u32[]{:S(2)}) collective-permute-start(f32[1,1024]{1,0:T(1,128)S(1)} %get-tuple-element.26), channel_id=1, source_target_pairs={{0,1},{1,0},{2,3},{3,2},{4,5},{5,4},{6,7},{7,6},{8,9},{9,8},{10,11... | collective-permute-start | bytes 12296 | tf_op jit(solution)/shard_map/ppermute | solution.py:332
  82.4 16.8 %collective-permute-start.4 = (f32[1,1024]{1,0:T(1,128)S(1)}, f32[1,1024]{1,0:T(1,128)S(1)}, u32[]{:S(2)}, u32[]{:S(2)}) collective-permute-start(f32[1,1024]{1,0:T(1,128)S(1)} %get-tuple-element.27), channel_id=1, source_target_pairs={{0,2},{1,3},{2,4},{3,5},{4,6},{5,7},{6,8},{7,9},{8,10},{9,11},{10,... | collective-permute-start | bytes 12296 | tf_op jit(solution)/shard_map/ppermute | solution.py:332
  94.2 7.0 %collective-permute-start.5 = (f32[1,1024]{1,0:T(1,128)S(1)}, f32[1,1024]{1,0:T(1,128)S(1)}, u32[]{:S(2)}, u32[]{:S(2)}) collective-permute-start(f32[1,1024]{1,0:T(1,128)S(1)} %get-tuple-element.28), channel_id=1, source_target_pairs={{0,4},{1,5},{2,6},{3,7},{4,8},{5,9},{6,10},{7,11},{8,12},{9,13},{1... | collective-permute-start | bytes 12296 | tf_op jit(solution)/shard_map/ppermute | solution.py:332

commit v4 on v3

--- a/solution.py
+++ b/solution.py
@@ -208,18 +208,33 @@
 CUTS = [slice(at, at + SIZE) for at in range(0, ROWS, SIZE)]
 
 
-def pair(a_ref, a_col, b_of, b_row, listed, row_acc, col_acc, total):
-    @pl.when(jnp.sum(listed) > 0.0)
+def pair(a_ref, a_col, b_of, b_row, row_acc, total):
+    over_rows = []
+    for part in CUTS:
+        b = b_of(part)
+        down = None
+        for at in CUTS:
+            by_row, by_col = tile_terms(nt(a_ref[at, :], b), a_col[at, :], b_row[:, part], False)
+            row_acc[at, :] = row_acc[at, :] + by_row
+            down = by_col if down is None else down + by_col
+        over_rows.append(down)
+    total[...] = total[...] + jnp.sum(jnp.concatenate(over_rows, axis=1), axis=0, keepdims=True)
+
+
+def listed_pairs(listed, first, second, between):
+    one, two = [jnp.sum(entry) > 0.0 for entry in listed]
+
+    @pl.when(one & two)
     def _():
-        for part in CUTS:
-            b = b_of(part)
-            down = None
-            for at in CUTS:
-                by_row, by_col = tile_terms(nt(a_ref[at, :], b), a_col[at, :], b_row[:, part], False)
-                row_acc[at, :] = row_acc[at, :] + by_row
-                down = by_col if down is None else down + by_col
-            col_acc[:, part] = down
-        total[...] = total[...] + jnp.sum(col_acc[...], axis=0, keepdims=True)
+        first()
+        between()
+        second()
+
+    @pl.when(jnp.logical_not(one & two))
+    def _():
+        pl.when(one)(first)
+        between()
+        pl.when(two)(second)
 
 
 def own_pair(ref, a_col, row, row_acc, col_acc):
@@ -238,16 +253,24 @@
     return jnp.sum(jnp.transpose(acc[...]), axis=0, keepdims=True)
 
 
-def first_kernel(got_hbm, own_ref, near_ref, ids_ref, sums_ref, far_ref, col, row_acc, col_acc, sems):
+def first_kernel(got_hbm, own_ref, near_ref, ids_ref, sums_ref, far_ref, col, row_acc, sems):
     rows = [tiles(got_hbm, c, far_ref.at[c - 1], sems.at[c]) for c in range(COPIES - 1, 0, -1)]
     col[...] = as_column(ids_ref[0])
     row_acc[...] = jnp.zeros_like(row_acc)
     sums_ref[...] = jnp.zeros_like(sums_ref)
-    for c in range(1, COPIES):
-        block = block_part(near_ref, 1) if c == 1 else block_part(far_ref, 1)
-        pair(own_ref, col, block, ids_ref[c], weight_of(own_ref, APART * c), row_acc, col_acc, sums_ref.at[c])
-        for copy in rows.pop(0):
+
+    def against(c, block):
+        return lambda: pair(own_ref, col, block, ids_ref[c], row_acc, sums_ref.at[c])
+
+    def arrived(copies):
+        for copy in copies:
             copy.wait()
+
+    listed = [weight_of(own_ref, APART * c) for c in range(1, COPIES)]
+    listed_pairs(
+        listed, against(1, block_part(near_ref, 1)), against(2, block_part(far_ref, 1)), lambda: arrived(rows[0])
+    )
+    arrived(rows[1])
     sums_ref[0] = fold_rows(row_acc)
 
 
@@ -271,16 +294,20 @@
 
 
 def second_kernel(core_ref, near_ref, far_ref, ids_ref, sums_ref, sw_ref, *refs):
-    outs, (total, col, row_acc, col_acc) = refs[:COPIES + 1], refs[COPIES + 1:]
+    outs, (total, col, row_acc) = refs[:COPIES + 1], refs[COPIES + 1:]
     total[...] = sums_ref[...]
     col[...] = as_column(ids_row(sw_ref))
     row_acc[...] = jnp.zeros_like(row_acc)
-    for n in range(2):
-        which = 1 - core_ref[0] + n
-        pair(
-            sw_ref, col, block_part(far_ref if n else near_ref, 1 - core_ref[0]), ids_ref[which], weight_of(sw_ref, 1 + 2 * n), row_acc,
-            col_acc, total.at[which],
-        )
+
+    def against(n, blocks_ref):
+        def run():
+            which = 1 - core_ref[0] + n
+            pair(sw_ref, col, block_part(blocks_ref, 1 - core_ref[0]), ids_ref[which], row_acc, total.at[which])
+
+        return run
+
+    listed = [weight_of(sw_ref, 1), weight_of(sw_ref, 3)]
+    listed_pairs(listed, against(0, near_ref), against(1, far_ref), lambda: None)
     for c in range(COPIES):
         outs[c][...] = total[c]
     outs[COPIES][...] = fold_rows(row_acc)
@@ -369,11 +396,11 @@
     sides = [scratch((ROWS, LANES), F32)] * 2 + [scratch((8, ROWS), F32)]
     sums, far = call(
         first_kernel, [jax.ShapeDtypeStruct((COPIES, 1, ROWS), F32), two_blocks], [ANY] + [VMEM] * 3,
-        sides + [sems((COPIES, PIECES))], 2, (got, own, near, block_ids), 16,
+        sides[:2] + [sems((COPIES, PIECES))], 2, (got, own, near, block_ids), 16,
     )
     sums = call(
         second_kernel, [vec(ROWS)] * (COPIES + 1), [SMEM] + [VMEM] * 5,
-        [scratch((COPIES, 1, ROWS), F32)] + sides,
+        [scratch((COPIES, 1, ROWS), F32)] + sides[:2],
         2, (core, near, far, block_ids, sums, sw), 16,
     )
     own_sum, place = call(

time: 103 us -> 103 us (level); the launches traced: 102 us -> 101 us
  starting transfers between devices: 34.5 us -> 30.8 us
  Pallas kernels: 13.6 us -> 16 us
    ppermute x6, starting transfers between devices: 23.2 us -> 19.4 us  [move(): return lax.ppermute(value, AXES, pairs)]
    pallas_call x6, Pallas kernels: 13.6 us -> 16 us  [call(): pl.pallas_call(kernel, out_shape=out_shape, in_specs=in_specs, out_specs=...]
  transfers between devices with their start and end apart: 7 -> 7, of which waited for: 4 -> 3; matrix products, arithmetic and copies ran while one was open for 0% -> 0% of each run, Pallas kernels for 4% -> 7%
where the time goes in v4:
time: 103 us; the launch traced here: 101 us
  waiting for transfers between devices  54.1 us (53%)
  starting transfers between devices  30.8 us (30%)
  Pallas kernels  16 us (16%)
    ppermute x6, waiting for transfers between devices, move(): return lax.ppermute(value, AXES, pairs)  54.1 us
    ppermute x6, starting transfers between devices, move(): return lax.ppermute(value, AXES, pairs)  19.4 us
    pallas_call x6, Pallas kernels, call(): pl.pallas_call(kernel, out_shape=out_shape, in_specs=in_specs, out_specs=...  16 us
    all_to_all x1, starting transfers between devices, local(): lax.all_to_all(outgoing, AXES, split_axis=0, concat_axis=0, tiled=True)  11.4 us
  transfers between devices with their start and end apart: 7, of which 3 were waited for; matrix products, arithmetic and copies ran while one was open for 0% of the time, Pallas kernels for 7%

profile of v4, /device:TPU:24, one launch (start us, length us, event | category | flops | bytes accessed | tf_op | source)
XLA Modules:
  0.0 101.0 jit_solution(5660344169630093317)
XLA Ops:
  0.0 5.2 %shard_map.46 = bf16[64,296,128]{2,1,0:T(8,128)(2,1)} custom-call(s32[1,1024]{1,0:T(1,128)} %bitcast.7, bf16[1024,768]{1,0:T(8,128)(2,1)} %emb_ref.1), custom_call_target="tpu_custom_call" | custom-call | flops 32212254720 | bytes 62914560 | tf_op jit(solution)/shard_map/pallas_call | solution.py:338
  5.2 0.0 copy-start
  5.3 0.0 copy-start.1
  5.3 11.4 %all-to-all-start = ((bf16[64,296,128]{2,1,0:T(8,128)(2,1)}), bf16[64,296,128]{2,1,0:T(8,128)(2,1)}, u32[]{:S(2)}, u32[]{:S(2)}) async-start(bf16[64,296,128]{2,1,0:T(8,128)(2,1)} %shard_map.46), calls=%async_computation | async-start | bytes 9699328 | tf_op jit(solution)/shard_map/all_to_all | solution.py:377
  16.6 0.0 copy-done
  16.6 2.8 %collective-permute-start = (s32[1,1024]{1,0:T(1,128)S(1)}, s32[1,1024]{1,0:T(1,128)S(1)}, u32[]{:S(2)}, u32[]{:S(2)}) collective-permute-start(s32[1,1024]{1,0:T(1,128)S(1)} %bitcast.4), channel_id=1, source_target_pairs={{2,0},{3,1},{4,2},{5,3},{6,4},{7,5},{8,6},{9,7},{10,8},{11,9},{12,... | collective-permute-start | bytes 12296 | tf_op jit(solution)/shard_map/ppermute | solution.py:359
  19.4 3.0 %collective-permute-start.1 = (s32[1,1024]{1,0:T(1,128)S(1)}, s32[1,1024]{1,0:T(1,128)S(1)}, u32[]{:S(2)}, u32[]{:S(2)}) collective-permute-start(s32[1,1024]{1,0:T(1,128)S(1)} %bitcast.5), channel_id=1, source_target_pairs={{4,0},{5,1},{6,2},{7,3},{8,4},{9,5},{10,6},{11,7},{12,8},{13,9},{1... | collective-permute-start | bytes 12296 | tf_op jit(solution)/shard_map/ppermute | solution.py:359
  22.5 0.0 copy-done.1
  22.5 50.0 %collective-permute-done.refs_1_ = s32[1,1024]{1,0:T(1,128)S(1)} collective-permute-done((s32[1,1024]{1,0:T(1,128)S(1)}, s32[1,1024]{1,0:T(1,128)S(1)}, u32[]{:S(2)}, u32[]{:S(2)}) %collective-permute-start) | collective-permute-done | bytes 4128 | tf_op jit(solution)/shard_map/ppermute | solution.py:359
  72.5 0.9 collective-permute-done.1.refs_2_
  73.4 0.0 all-to-all-done.got_hbm
  73.4 2.3 %shard_map.47 = (bf16[1040,768]{1,0:T(8,128)(2,1)S(1)}, bf16[2,64,16,768]{3,2,1,0:T(8,128)(2,1)S(1)}, f32[3,1,1024]{2,1,0:T(1,128)S(1)}, s32[1,1024]{1,0:T(1,128)S(1)}) custom-call(bf16[64,296,128]{2,1,0:T(8,128)(2,1)} %all-to-all-done.got_hbm, s32[1,128]{1,0:T(1,128)S(1)} %pad.4.list_ref, s32[1,1024]{1,0:T(1,128)S(1)} %bitcast.6, ...), custom_call_target="tpu_custom_call" | custom-call | flops 16106127360 | bytes 47185920 | tf_op jit(solution)/shard_map/pallas_call | solution.py:338
  75.7 0.1 collective-permute-start.2
  75.8 4.9 %shard_map.48 = (f32[3,1,1024]{2,1,0:T(1,128)S(1)}, bf16[2,64,16,768]{3,2,1,0:T(8,128)(2,1)S(1)}) custom-call(bf16[64,296,128]{2,1,0:T(8,128)(2,1)} %all-to-all-done.got_hbm, bf16[1040,768]{1,0:T(8,128)(2,1)S(1)} %get-tuple-element.17.own_ref, bf16[2,64,16,768]{3,2,1,0:T(8,128)(2,1)S(1)} %get-tuple-element.19.near_ref, ...), custom_call_target="tpu_custom_call" | custom-call | flops 64424509440 | bytes 94371840 | tf_op jit(solution)/shard_map/pallas_call | solution.py:338
  80.7 0.0 collective-permute-done.2.sw_ref
  80.7 0.5 shard_map.49
  81.1 0.5 collective-permute-start.3
  81.7 11.1 %collective-permute-start.4 = (f32[1,1024]{1,0:T(1,128)S(1)}, f32[1,1024]{1,0:T(1,128)S(1)}, u32[]{:S(2)}, u32[]{:S(2)}) collective-permute-start(f32[1,1024]{1,0:T(1,128)S(1)} %get-tuple-element.27), channel_id=1, source_target_pairs={{0,2},{1,3},{2,4},{3,5},{4,6},{5,7},{6,8},{7,9},{8,10},{9,11},{10,... | collective-permute-start | bytes 12296 | tf_op jit(solution)/shard_map/ppermute | solution.py:359
  92.7 1.9 %collective-permute-start.5 = (f32[1,1024]{1,0:T(1,128)S(1)}, f32[1,1024]{1,0:T(1,128)S(1)}, u32[]{:S(2)}, u32[]{:S(2)}) collective-permute-start(f32[1,1024]{1,0:T(1,128)S(1)} %get-tuple-element.28), channel_id=1, source_target_pairs={{0,4},{1,5},{2,6},{3,7},{4,8},{5,9},{6,10},{7,11},{8,12},{9,13},{1... | collective-permute-start | bytes 12296 | tf_op jit(solution)/shard_map/ppermute | solution.py:359
  94.7 1.8 %shard_map.50 = (f32[1,1024]{1,0:T(1,128)S(1)}, bf16[1024,1024]{1,0:T(8,128)(2,1)S(1)}) custom-call(bf16[1040,768]{1,0:T(8,128)(2,1)S(1)} %get-tuple-element.17.own_ref, s32[1,1024]{1,0:T(1,128)S(1)} %get-tuple-element.18.land_ref, f32[1,1024]{1,0:T(1,128)S(1)} %get-tuple-element.23.sum_ref), custom_call_target="tpu_custom_call" | custom-call | flops 19327352832 | bytes 50331648 | tf_op jit(solution)/shard_map/pallas_call | solution.py:338
  96.5 0.0 collective-permute-done.3.refs_1_
  96.5 0.0 collective-permute-done.4.refs_2_
  96.5 3.2 %collective-permute-done.5.refs_3_ = f32[1,1024]{1,0:T(1,128)S(1)} collective-permute-done((f32[1,1024]{1,0:T(1,128)S(1)}, f32[1,1024]{1,0:T(1,128)S(1)}, u32[]{:S(2)}, u32[]{:S(2)}) %collective-permute-start.5) | collective-permute-done | bytes 4128 | tf_op jit(solution)/shard_map/ppermute | solution.py:359
  99.7 1.3 %shard_map.51 = f32[1,1024]{1,0:T(1,128)} custom-call(bf16[1024,1024]{1,0:T(8,128)(2,1)S(1)} %get-tuple-element.24.place_ref, f32[1,1024]{1,0:T(1,128)S(1)} %get-tuple-element.25.refs_0_, f32[1,1024]{1,0:T(1,128)S(1)} %collective-permute-done.3.refs_1_, f32[1,1024]{1,0:T(1,128)S(1)} %collective-permute-done.4.refs_2_, ...), custom_call_target="tpu_custom_call" | custom-call | flops 6442450944 | bytes 37748736 | tf_op jit(solution)/shard_map/pallas_call | solution.py:338
  (2 shorter events, 0.0 us)
Async XLA Ops:
  5.2 11.4 %copy-start = (s32[1024]{0:T(1024)S(1)}, s32[1024]{0:T(1024)}, u32[]{:S(2)}) copy-start(s32[1024]{0:T(1024)} %param.6) | copy-start | bytes 12292
  5.3 17.2 %copy-start.1 = (s32[1,4]{1,0:T(1,128)S(1)}, s32[1,4]{1,0:T(1,128)}, u32[]{:S(2)}) copy-start(s32[1,4]{1,0:T(1,128)} %param.7) | copy-start | bytes 52
  5.3 68.1 %all-to-all-start = ((bf16[64,296,128]{2,1,0:T(8,128)(2,1)}), bf16[64,296,128]{2,1,0:T(8,128)(2,1)}, u32[]{:S(2)}, u32[]{:S(2)}) async-start(bf16[64,296,128]{2,1,0:T(8,128)(2,1)} %shard_map.46), calls=%async_computation | async-start | bytes 9699328 | tf_op jit(solution)/shard_map/all_to_all | solution.py:377
  16.6 55.8 %collective-permute-start = (s32[1,1024]{1,0:T(1,128)S(1)}, s32[1,1024]{1,0:T(1,128)S(1)}, u32[]{:S(2)}, u32[]{:S(2)}) collective-permute-start(s32[1,1024]{1,0:T(1,128)S(1)} %bitcast.4), channel_id=1, source_target_pairs={{2,0},{3,1},{4,2},{5,3},{6,4},{7,5},{8,6},{9,7},{10,8},{11,9},{12,... | collective-permute-start | bytes 12296 | tf_op jit(solution)/shard_map/ppermute | solution.py:359
  19.4 54.0 %collective-permute-start.1 = (s32[1,1024]{1,0:T(1,128)S(1)}, s32[1,1024]{1,0:T(1,128)S(1)}, u32[]{:S(2)}, u32[]{:S(2)}) collective-permute-start(s32[1,1024]{1,0:T(1,128)S(1)} %bitcast.5), channel_id=1, source_target_pairs={{4,0},{5,1},{6,2},{7,3},{8,4},{9,5},{10,6},{11,7},{12,8},{13,9},{1... | collective-permute-start | bytes 12296 | tf_op jit(solution)/shard_map/ppermute | solution.py:359
  75.7 5.0 %collective-permute-start.2 = (bf16[1040,768]{1,0:T(8,128)(2,1)S(1)}, bf16[1040,768]{1,0:T(8,128)(2,1)S(1)}, u32[]{:S(2)}, u32[]{:S(2)}) collective-permute-start(bf16[1040,768]{1,0:T(8,128)(2,1)S(1)} %get-tuple-element.17.own_ref), channel_id=1, source_target_pairs={{0,1},{1,0},{2,3},{3,2},{4,5},{5,4},{6,7},{7,6},{8,9},{9,8},{10,11... | collective-permute-start | bytes 4792328 | tf_op jit(solution)/shard_map/ppermute | solution.py:359
  81.1 15.4 %collective-permute-start.3 = (f32[1,1024]{1,0:T(1,128)S(1)}, f32[1,1024]{1,0:T(1,128)S(1)}, u32[]{:S(2)}, u32[]{:S(2)}) collective-permute-start(f32[1,1024]{1,0:T(1,128)S(1)} %get-tuple-element.26), channel_id=1, source_target_pairs={{0,1},{1,0},{2,3},{3,2},{4,5},{5,4},{6,7},{7,6},{8,9},{9,8},{10,11... | collective-permute-start | bytes 12296 | tf_op jit(solution)/shard_map/ppermute | solution.py:359
  81.7 14.9 %collective-permute-start.4 = (f32[1,1024]{1,0:T(1,128)S(1)}, f32[1,1024]{1,0:T(1,128)S(1)}, u32[]{:S(2)}, u32[]{:S(2)}) collective-permute-start(f32[1,1024]{1,0:T(1,128)S(1)} %get-tuple-element.27), channel_id=1, source_target_pairs={{0,2},{1,3},{2,4},{3,5},{4,6},{5,7},{6,8},{7,9},{8,10},{9,11},{10,... | collective-permute-start | bytes 12296 | tf_op jit(solution)/shard_map/ppermute | solution.py:359
  92.7 7.0 %collective-permute-start.5 = (f32[1,1024]{1,0:T(1,128)S(1)}, f32[1,1024]{1,0:T(1,128)S(1)}, u32[]{:S(2)}, u32[]{:S(2)}) collective-permute-start(f32[1,1024]{1,0:T(1,128)S(1)} %get-tuple-element.28), channel_id=1, source_target_pairs={{0,4},{1,5},{2,6},{3,7},{4,8},{5,9},{6,10},{7,11},{8,12},{9,13},{1... | collective-permute-start | bytes 12296 | tf_op jit(solution)/shard_map/ppermute | solution.py:359

commit v5 on v4

--- a/solution.py
+++ b/solution.py
@@ -159,7 +159,7 @@
 def split_kernel(got_hbm, list_ref, *refs):
     ids_refs, (out_ref, blocks_ref, far_ref, land_ref, digit_ref, sems) = refs[:COPIES], refs[COPIES:]
     slots = slot_tiles(got_hbm, digit_ref, sems.at[0, PIECES])
-    rows = [tiles(got_hbm, c, blocks_ref.at[c], sems.at[c]) for c in range(COPIES - 1)]
+    rows = [tiles(got_hbm, c, blocks_ref.at[c], sems.at[c]) for c in range(COPIES)]
     slots.wait()
     lands = arrival_slots(digit_ref[...], range(COPIES))
     land_ref[...] = lands[0]
@@ -175,7 +175,7 @@
     for copy in rows[0]:
         copy.wait()
     out_ref[0:ROWS, :] = blocks_ref[0].reshape(ROWS, WIDTH)
-    for copy in rows[1]:
+    for copy in (*rows[1], *rows[2]):
         copy.wait()
 
 
@@ -221,19 +221,17 @@
     total[...] = total[...] + jnp.sum(jnp.concatenate(over_rows, axis=1), axis=0, keepdims=True)
 
 
-def listed_pairs(listed, first, second, between):
+def listed_pairs(listed, first, second):
     one, two = [jnp.sum(entry) > 0.0 for entry in listed]
 
     @pl.when(one & two)
     def _():
         first()
-        between()
         second()
 
     @pl.when(jnp.logical_not(one & two))
     def _():
         pl.when(one)(first)
-        between()
         pl.when(two)(second)
 
 
@@ -253,30 +251,19 @@
     return jnp.sum(jnp.transpose(acc[...]), axis=0, keepdims=True)
 
 
-def first_kernel(got_hbm, own_ref, near_ref, ids_ref, sums_ref, far_ref, col, row_acc, sems):
-    rows = [tiles(got_hbm, c, far_ref.at[c - 1], sems.at[c]) for c in range(COPIES - 1, 0, -1)]
+def first_kernel(own_ref, blocks_ref, ids_ref, sums_ref, col, row_acc):
     col[...] = as_column(ids_ref[0])
     row_acc[...] = jnp.zeros_like(row_acc)
     sums_ref[...] = jnp.zeros_like(sums_ref)
 
-    def against(c, block):
-        return lambda: pair(own_ref, col, block, ids_ref[c], row_acc, sums_ref.at[c])
-
-    def arrived(copies):
-        for copy in copies:
-            copy.wait()
-
-    listed = [weight_of(own_ref, APART * c) for c in range(1, COPIES)]
-    listed_pairs(
-        listed, against(1, block_part(near_ref, 1)), against(2, block_part(far_ref, 1)), lambda: arrived(rows[0])
-    )
-    arrived(rows[1])
+    def against(c):
+        return lambda: pair(own_ref, col, block_part(blocks_ref, c), ids_ref[c], row_acc, sums_ref.at[c])
+
+    listed_pairs([weight_of(own_ref, APART * c) for c in range(1, COPIES)], against(1), against(2))
     sums_ref[0] = fold_rows(row_acc)
 
 
-def self_kernel(own_ref, land_ref, sum_ref, out_ref, place_ref, col, row_acc, col_acc):
-    for at in range(0, ROWS, 256):
-        place_ref[at:at + 256, :] = one_hot(256, at, land_ref[...])
+def self_kernel(own_ref, sum_ref, out_ref, col, row_acc, col_acc):
     row = ids_row(own_ref)
     col[...] = as_column(row)
     row_acc[...] = jnp.zeros_like(row_acc)
@@ -293,27 +280,26 @@
     return part
 
 
-def second_kernel(core_ref, near_ref, far_ref, ids_ref, sums_ref, sw_ref, *refs):
+def second_kernel(core_ref, blocks_ref, ids_ref, sums_ref, sw_ref, *refs):
     outs, (total, col, row_acc) = refs[:COPIES + 1], refs[COPIES + 1:]
     total[...] = sums_ref[...]
     col[...] = as_column(ids_row(sw_ref))
     row_acc[...] = jnp.zeros_like(row_acc)
 
-    def against(n, blocks_ref):
+    def against(n):
         def run():
             which = 1 - core_ref[0] + n
-            pair(sw_ref, col, block_part(blocks_ref, 1 - core_ref[0]), ids_ref[which], row_acc, total.at[which])
+            pair(sw_ref, col, block_part(blocks_ref, which), ids_ref[which], row_acc, total.at[which])
 
         return run
 
-    listed = [weight_of(sw_ref, 1), weight_of(sw_ref, 3)]
-    listed_pairs(listed, against(0, near_ref), against(1, far_ref), lambda: None)
+    listed_pairs([weight_of(sw_ref, 1), weight_of(sw_ref, 3)], against(0), against(1))
     for c in range(COPIES):
         outs[c][...] = total[c]
     outs[COPIES][...] = fold_rows(row_acc)
 
 
-def end_kernel(place_ref, *refs):
+def end_kernel(land_ref, *refs):
     out_ref = refs[-1]
     load = refs[0][...]
     for ref in refs[1:-1]:
@@ -325,7 +311,7 @@
     which = iota((8, ROWS), 0)
     parts = jnp.where(which == 0, high, jnp.where(which == 1, mid, jnp.where(which == 2, low, 0.0))).astype(BF16)
     for step in range(4):
-        placed = nt(parts, place_ref[step * 256:(step + 1) * 256, :])
+        placed = nt(parts, one_hot(256, step * 256, land_ref[...]))
         out_ref[:, step * 256:(step + 1) * 256] = placed[0:1, :] + placed[1:2, :] + placed[2:3, :]
 
 
@@ -380,12 +366,11 @@
     reach = position + 1 + jnp.arange(SHIFTS, dtype=jnp.int32)
     entries = jnp.pad(jnp.where(reach[None, :] < devices, block_list, 0), ((0, 0), (0, LANES - SHIFTS)))
     sems = pltpu.SemaphoreType.DMA
-    two_blocks = jax.ShapeDtypeStruct((2, devices, PER_PAIR, WIDTH), BF16)
-    own, near, block_ids, land = call(
+    own, blocks, block_ids, land = call(
         split_kernel,
         [
             jax.ShapeDtypeStruct((ROWS + TAIL, WIDTH), BF16),
-            two_blocks,
+            jax.ShapeDtypeStruct((COPIES, devices, PER_PAIR, WIDTH), BF16),
             jax.ShapeDtypeStruct((COPIES, 1, ROWS), F32),
             jax.ShapeDtypeStruct((1, ROWS), jnp.int32),
         ],
@@ -394,22 +379,18 @@
     )
     sw = move_d(own, change=lambda p: p ^ 1)
     sides = [scratch((ROWS, LANES), F32)] * 2 + [scratch((8, ROWS), F32)]
-    sums, far = call(
-        first_kernel, [jax.ShapeDtypeStruct((COPIES, 1, ROWS), F32), two_blocks], [ANY] + [VMEM] * 3,
-        sides[:2] + [sems((COPIES, PIECES))], 2, (got, own, near, block_ids), 16,
+    sums = call(
+        first_kernel, jax.ShapeDtypeStruct((COPIES, 1, ROWS), F32), [VMEM] * 3, sides[:2], 2, (own, blocks, block_ids), 16
     )
     sums = call(
-        second_kernel, [vec(ROWS)] * (COPIES + 1), [SMEM] + [VMEM] * 5,
+        second_kernel, [vec(ROWS)] * (COPIES + 1), [SMEM] + [VMEM] * 4,
         [scratch((COPIES, 1, ROWS), F32)] + sides[:2],
-        2, (core, near, far, block_ids, sums, sw), 16,
+        2, (core, blocks, block_ids, sums, sw), 16,
     )
-    own_sum, place = call(
-        self_kernel, [vec(ROWS), jax.ShapeDtypeStruct((ROWS, ROWS), BF16)], [VMEM] * 3, sides,
-        0.6, (own, land, sums[0]), 16,
-    )
+    own_sum = call(self_kernel, vec(ROWS), [VMEM] * 2, sides, 0.6, (own, sums[0]), 16)
     returned = [own_sum, move_d(sums[COPIES], change=lambda p: p ^ 1)]
     returned += [move_d(sums[c], change=lambda p, c=c: p + APART * c) for c in range(1, COPIES)]
-    weights = call(end_kernel, vec(ROWS), [VMEM] * (COPIES + 2), [], 0.2, (place, *returned))
+    weights = call(end_kernel, vec(ROWS), [VMEM] * (COPIES + 2), [], 0.2, (land, *returned))
     return weights.reshape(ROWS)
 
 

time: 103 us -> 101 us (0.981)
  the two profiles are of different devices: /device:TPU:24 before, /device:TPU:34 now
where the time goes in v5:
time: 101 us; the launch traced here: 99.7 us
  waiting for transfers between devices  54.4 us (54%)
  starting transfers between devices  29.4 us (29%)
  Pallas kernels  15.7 us (16%)
    ppermute x6, waiting for transfers between devices, move(): return lax.ppermute(value, AXES, pairs)  50.6 us
    ppermute x6, starting transfers between devices, move(): return lax.ppermute(value, AXES, pairs)  19 us
    pallas_call x6, Pallas kernels, call(): pl.pallas_call(kernel, out_shape=out_shape, in_specs=in_specs, out_specs=...  15.7 us
    all_to_all x1, starting transfers between devices, local(): lax.all_to_all(outgoing, AXES, split_axis=0, concat_axis=0, tiled=True)  10.4 us
    all_to_all x1, waiting for transfers between devices, local(): lax.all_to_all(outgoing, AXES, split_axis=0, concat_axis=0, tiled=True)  3.85 us
  transfers between devices with their start and end apart: 7, of which 4 were waited for; matrix products, arithmetic and copies ran while one was open for 0% of the time, Pallas kernels for 6%

profile of v5, /device:TPU:34, one launch (start us, length us, event | category | flops | bytes accessed | tf_op | source)
XLA Modules:
  0.0 99.7 jit_solution(3083539282324206337)
XLA Ops:
  0.0 5.2 %shard_map.46 = bf16[64,296,128]{2,1,0:T(8,128)(2,1)} custom-call(s32[1,1024]{1,0:T(1,128)} %bitcast.7, bf16[1024,768]{1,0:T(8,128)(2,1)} %emb_ref.1), custom_call_target="tpu_custom_call" | custom-call | flops 32212254720 | bytes 62914560 | tf_op jit(solution)/shard_map/pallas_call | solution.py:324
  5.3 0.0 copy-start
  5.3 0.0 copy-start.1
  5.3 10.4 %all-to-all-start = ((bf16[64,296,128]{2,1,0:T(8,128)(2,1)}), bf16[64,296,128]{2,1,0:T(8,128)(2,1)}, u32[]{:S(2)}, u32[]{:S(2)}) async-start(bf16[64,296,128]{2,1,0:T(8,128)(2,1)} %shard_map.46), calls=%async_computation | async-start | bytes 9699328 | tf_op jit(solution)/shard_map/all_to_all | solution.py:363
  15.6 0.0 copy-done
  15.6 7.3 %collective-permute-start.1 = (s32[1,1024]{1,0:T(1,128)S(1)}, s32[1,1024]{1,0:T(1,128)S(1)}, u32[]{:S(2)}, u32[]{:S(2)}) collective-permute-start(s32[1,1024]{1,0:T(1,128)S(1)} %bitcast.4), channel_id=1, source_target_pairs={{4,0},{5,1},{6,2},{7,3},{8,4},{9,5},{10,6},{11,7},{12,8},{13,9},{1... | collective-permute-start | bytes 12296 | tf_op jit(solution)/shard_map/ppermute | solution.py:345
  22.9 3.1 %collective-permute-start = (s32[1,1024]{1,0:T(1,128)S(1)}, s32[1,1024]{1,0:T(1,128)S(1)}, u32[]{:S(2)}, u32[]{:S(2)}) collective-permute-start(s32[1,1024]{1,0:T(1,128)S(1)} %bitcast.5), channel_id=1, source_target_pairs={{2,0},{3,1},{4,2},{5,3},{6,4},{7,5},{8,6},{9,7},{10,8},{11,9},{12,... | collective-permute-start | bytes 12296 | tf_op jit(solution)/shard_map/ppermute | solution.py:345
  26.0 0.0 copy-done.1
  26.1 43.7 %collective-permute-done.1.refs_2_ = s32[1,1024]{1,0:T(1,128)S(1)} collective-permute-done((s32[1,1024]{1,0:T(1,128)S(1)}, s32[1,1024]{1,0:T(1,128)S(1)}, u32[]{:S(2)}, u32[]{:S(2)}) %collective-permute-start.1) | collective-permute-done | bytes 4128 | tf_op jit(solution)/shard_map/ppermute | solution.py:345
  69.8 0.0 collective-permute-done.refs_1_
  69.8 3.9 %all-to-all-done.got_hbm = bf16[64,296,128]{2,1,0:T(8,128)(2,1)} async-done(((bf16[64,296,128]{2,1,0:T(8,128)(2,1)}), bf16[64,296,128]{2,1,0:T(8,128)(2,1)}, u32[]{:S(2)}, u32[]{:S(2)}) %all-to-all-start) | async-done | bytes 4849696 | tf_op jit(solution)/shard_map/all_to_all | solution.py:363
  73.6 2.6 %shard_map.47 = (bf16[1040,768]{1,0:T(8,128)(2,1)S(1)}, bf16[3,64,16,768]{3,2,1,0:T(8,128)(2,1)S(1)}, f32[3,1,1024]{2,1,0:T(1,128)S(1)}, s32[1,1024]{1,0:T(1,128)S(1)}) custom-call(bf16[64,296,128]{2,1,0:T(8,128)(2,1)} %all-to-all-done.got_hbm, s32[1,128]{1,0:T(1,128)S(1)} %pad.4.list_ref, s32[1,1024]{1,0:T(1,128)S(1)} %bitcast.6, ...), custom_call_target="tpu_custom_call" | custom-call | flops 16106127360 | bytes 47185920 | tf_op jit(solution)/shard_map/pallas_call | solution.py:324
  76.3 2.0 %collective-permute-start.2 = (bf16[1040,768]{1,0:T(8,128)(2,1)S(1)}, bf16[1040,768]{1,0:T(8,128)(2,1)S(1)}, u32[]{:S(2)}, u32[]{:S(2)}) collective-permute-start(bf16[1040,768]{1,0:T(8,128)(2,1)S(1)} %get-tuple-element.14.own_ref), channel_id=1, source_target_pairs={{0,1},{1,0},{2,3},{3,2},{4,5},{5,4},{6,7},{7,6},{8,9},{9,8},{10,11... | collective-permute-start | bytes 4792328 | tf_op jit(solution)/shard_map/ppermute | solution.py:345
  78.2 4.6 %shard_map.48.sums_ref = f32[3,1,1024]{2,1,0:T(1,128)S(1)} custom-call(bf16[1040,768]{1,0:T(8,128)(2,1)S(1)} %get-tuple-element.14.own_ref, bf16[3,64,16,768]{3,2,1,0:T(8,128)(2,1)S(1)} %get-tuple-element.15.blocks_ref, f32[3,1,1024]{2,1,0:T(1,128)S(1)} %get-tuple-element.16.ids_ref), custom_call_target="tpu_custom_call" | custom-call | flops 64424509440 | bytes 94371840 | tf_op jit(solution)/shard_map/pallas_call | solution.py:324
  82.8 0.0 collective-permute-done.2.sw_ref
  82.9 0.5 shard_map.49
  83.3 1.0 collective-permute-start.3
  84.3 3.8 %collective-permute-start.4 = (f32[1,1024]{1,0:T(1,128)S(1)}, f32[1,1024]{1,0:T(1,128)S(1)}, u32[]{:S(2)}, u32[]{:S(2)}) collective-permute-start(f32[1,1024]{1,0:T(1,128)S(1)} %get-tuple-element.19), channel_id=1, source_target_pairs={{0,2},{1,3},{2,4},{3,5},{4,6},{5,7},{6,8},{7,9},{8,10},{9,11},{10,... | collective-permute-start | bytes 12296 | tf_op jit(solution)/shard_map/ppermute | solution.py:345
  88.1 1.9 %collective-permute-start.5 = (f32[1,1024]{1,0:T(1,128)S(1)}, f32[1,1024]{1,0:T(1,128)S(1)}, u32[]{:S(2)}, u32[]{:S(2)}) collective-permute-start(f32[1,1024]{1,0:T(1,128)S(1)} %get-tuple-element.20), channel_id=1, source_target_pairs={{0,4},{1,5},{2,6},{3,7},{4,8},{5,9},{6,10},{7,11},{8,12},{9,13},{1... | collective-permute-start | bytes 12296 | tf_op jit(solution)/shard_map/ppermute | solution.py:345
  90.0 1.5 %shard_map.50.refs_0_ = f32[1,1024]{1,0:T(1,128)S(1)} custom-call(bf16[1040,768]{1,0:T(8,128)(2,1)S(1)} %get-tuple-element.14.own_ref, f32[1,1024]{1,0:T(1,128)S(1)} %get-tuple-element.17.sum_ref), custom_call_target="tpu_custom_call" | custom-call | flops 19327352832 | bytes 50331648 | tf_op jit(solution)/shard_map/pallas_call | solution.py:324
  91.5 0.0 collective-permute-done.3.refs_1_
  91.5 2.8 %collective-permute-done.4.refs_2_ = f32[1,1024]{1,0:T(1,128)S(1)} collective-permute-done((f32[1,1024]{1,0:T(1,128)S(1)}, f32[1,1024]{1,0:T(1,128)S(1)}, u32[]{:S(2)}, u32[]{:S(2)}) %collective-permute-start.4) | collective-permute-done | bytes 4128 | tf_op jit(solution)/shard_map/ppermute | solution.py:345
  94.3 4.1 %collective-permute-done.5.refs_3_ = f32[1,1024]{1,0:T(1,128)S(1)} collective-permute-done((f32[1,1024]{1,0:T(1,128)S(1)}, f32[1,1024]{1,0:T(1,128)S(1)}, u32[]{:S(2)}, u32[]{:S(2)}) %collective-permute-start.5) | collective-permute-done | bytes 4128 | tf_op jit(solution)/shard_map/ppermute | solution.py:345
  98.4 1.3 %shard_map.51 = f32[1,1024]{1,0:T(1,128)} custom-call(s32[1,1024]{1,0:T(1,128)S(1)} %get-tuple-element.13.land_ref, f32[1,1024]{1,0:T(1,128)S(1)} %shard_map.50.refs_0_, f32[1,1024]{1,0:T(1,128)S(1)} %collective-permute-done.3.refs_1_, f32[1,1024]{1,0:T(1,128)S(1)} %collective-permute-done.4.refs_2_, f32[1,1024]{1,0:T(1,128)S(1)} %collective-permute-done.5.refs_3_), custom_call_target="tpu_custom_call" | custom-call | flops 6442450944 | bytes 37748736 | tf_op jit(solution)/shard_map/pallas_call | solution.py:324
  (2 shorter events, 0.0 us)
Async XLA Ops:
  5.3 10.4 %copy-start = (s32[1024]{0:T(1024)S(1)}, s32[1024]{0:T(1024)}, u32[]{:S(2)}) copy-start(s32[1024]{0:T(1024)} %param.6) | copy-start | bytes 12292
  5.3 20.8 %copy-start.1 = (s32[1,4]{1,0:T(1,128)S(1)}, s32[1,4]{1,0:T(1,128)}, u32[]{:S(2)}) copy-start(s32[1,4]{1,0:T(1,128)} %param.7) | copy-start | bytes 52
  5.3 68.3 %all-to-all-start = ((bf16[64,296,128]{2,1,0:T(8,128)(2,1)}), bf16[64,296,128]{2,1,0:T(8,128)(2,1)}, u32[]{:S(2)}, u32[]{:S(2)}) async-start(bf16[64,296,128]{2,1,0:T(8,128)(2,1)} %shard_map.46), calls=%async_computation | async-start | bytes 9699328 | tf_op jit(solution)/shard_map/all_to_all | solution.py:363
  15.6 54.1 %collective-permute-start.1 = (s32[1,1024]{1,0:T(1,128)S(1)}, s32[1,1024]{1,0:T(1,128)S(1)}, u32[]{:S(2)}, u32[]{:S(2)}) collective-permute-start(s32[1,1024]{1,0:T(1,128)S(1)} %bitcast.4), channel_id=1, source_target_pairs={{4,0},{5,1},{6,2},{7,3},{8,4},{9,5},{10,6},{11,7},{12,8},{13,9},{1... | collective-permute-start | bytes 12296 | tf_op jit(solution)/shard_map/ppermute | solution.py:345
  22.9 46.8 %collective-permute-start = (s32[1,1024]{1,0:T(1,128)S(1)}, s32[1,1024]{1,0:T(1,128)S(1)}, u32[]{:S(2)}, u32[]{:S(2)}) collective-permute-start(s32[1,1024]{1,0:T(1,128)S(1)} %bitcast.5), channel_id=1, source_target_pairs={{2,0},{3,1},{4,2},{5,3},{6,4},{7,5},{8,6},{9,7},{10,8},{11,9},{12,... | collective-permute-start | bytes 12296 | tf_op jit(solution)/shard_map/ppermute | solution.py:345
  76.3 6.6 %collective-permute-start.2 = (bf16[1040,768]{1,0:T(8,128)(2,1)S(1)}, bf16[1040,768]{1,0:T(8,128)(2,1)S(1)}, u32[]{:S(2)}, u32[]{:S(2)}) collective-permute-start(bf16[1040,768]{1,0:T(8,128)(2,1)S(1)} %get-tuple-element.14.own_ref), channel_id=1, source_target_pairs={{0,1},{1,0},{2,3},{3,2},{4,5},{5,4},{6,7},{7,6},{8,9},{9,8},{10,11... | collective-permute-start | bytes 4792328 | tf_op jit(solution)/shard_map/ppermute | solution.py:345
  83.3 8.2 %collective-permute-start.3 = (f32[1,1024]{1,0:T(1,128)S(1)}, f32[1,1024]{1,0:T(1,128)S(1)}, u32[]{:S(2)}, u32[]{:S(2)}) collective-permute-start(f32[1,1024]{1,0:T(1,128)S(1)} %get-tuple-element.18), channel_id=1, source_target_pairs={{0,1},{1,0},{2,3},{3,2},{4,5},{5,4},{6,7},{7,6},{8,9},{9,8},{10,11... | collective-permute-start | bytes 12296 | tf_op jit(solution)/shard_map/ppermute | solution.py:345
  84.3 10.0 %collective-permute-start.4 = (f32[1,1024]{1,0:T(1,128)S(1)}, f32[1,1024]{1,0:T(1,128)S(1)}, u32[]{:S(2)}, u32[]{:S(2)}) collective-permute-start(f32[1,1024]{1,0:T(1,128)S(1)} %get-tuple-element.19), channel_id=1, source_target_pairs={{0,2},{1,3},{2,4},{3,5},{4,6},{5,7},{6,8},{7,9},{8,10},{9,11},{10,... | collective-permute-start | bytes 12296 | tf_op jit(solution)/shard_map/ppermute | solution.py:345
  88.1 10.3 %collective-permute-start.5 = (f32[1,1024]{1,0:T(1,128)S(1)}, f32[1,1024]{1,0:T(1,128)S(1)}, u32[]{:S(2)}, u32[]{:S(2)}) collective-permute-start(f32[1,1024]{1,0:T(1,128)S(1)} %get-tuple-element.20), channel_id=1, source_target_pairs={{0,4},{1,5},{2,6},{3,7},{4,8},{5,9},{6,10},{7,11},{8,12},{9,13},{1... | collective-permute-start | bytes 12296 | tf_op jit(solution)/shard_map/ppermute | solution.py:345

commit v6 on v5

--- a/solution.py
+++ b/solution.py
@@ -196,7 +196,7 @@
         cut = slice(lane * LANES, (lane + 1) * LANES)
         half = jnp.tanh(scores[:, cut] * (0.5 * sharpness) - 0.5 * sharpness * threshold)
         factor = jnp.where(id_col == id_row[:, cut], 0.5, 0.25)
-        term = factor * (1.0 + half)
+        term = factor + factor * half
         if masked:
             term = jnp.where(iota(term.shape, 0) == iota(term.shape, 1) + lane * LANES, 0.0, term)
         over_cols = term if over_cols is None else over_cols + term

time: 101 us -> 102 us (level)
  transfers between devices with their start and end apart: 7 -> 7, of which waited for: 4 -> 5; matrix products, arithmetic and copies ran while one was open for 0% -> 0% of each run, Pallas kernels for 6% -> 4%
where the time goes in v6:
time: 102 us; the launch traced here: 99.6 us
  waiting for transfers between devices  53.9 us (53%)
  starting transfers between devices  29.8 us (29%)
  Pallas kernels  15.9 us (16%)
    ppermute x6, waiting for transfers between devices, move(): return lax.ppermute(value, AXES, pairs)  50 us
    ppermute x6, starting transfers between devices, move(): return lax.ppermute(value, AXES, pairs)  19.4 us
    pallas_call x6, Pallas kernels, call(): pl.pallas_call(kernel, out_shape=out_shape, in_specs=in_specs, out_specs=...  15.9 us
    all_to_all x1, starting transfers between devices, local(): lax.all_to_all(outgoing, AXES, split_axis=0, concat_axis=0, tiled=True)  10.4 us
    all_to_all x1, waiting for transfers between devices, local(): lax.all_to_all(outgoing, AXES, split_axis=0, concat_axis=0, tiled=True)  3.85 us
  transfers between devices with their start and end apart: 7, of which 5 were waited for; matrix products, arithmetic and copies ran while one was open for 0% of the time, Pallas kernels for 4%

profile of v6, /device:TPU:34, one launch (start us, length us, event | category | flops | bytes accessed | tf_op | source)
XLA Modules:
  0.0 99.6 jit_solution(1183291194769564548)
XLA Ops:
  0.0 5.2 %shard_map.46 = bf16[64,296,128]{2,1,0:T(8,128)(2,1)} custom-call(s32[1,1024]{1,0:T(1,128)} %bitcast.7, bf16[1024,768]{1,0:T(8,128)(2,1)} %emb_ref.1), custom_call_target="tpu_custom_call" | custom-call | flops 32212254720 | bytes 62914560 | tf_op jit(solution)/shard_map/pallas_call | solution.py:324
  5.3 0.0 copy-start
  5.3 0.0 copy-start.1
  5.3 10.4 %all-to-all-start = ((bf16[64,296,128]{2,1,0:T(8,128)(2,1)}), bf16[64,296,128]{2,1,0:T(8,128)(2,1)}, u32[]{:S(2)}, u32[]{:S(2)}) async-start(bf16[64,296,128]{2,1,0:T(8,128)(2,1)} %shard_map.46), calls=%async_computation | async-start | bytes 9699328 | tf_op jit(solution)/shard_map/all_to_all | solution.py:363
  15.6 0.0 copy-done
  15.6 7.3 %collective-permute-start.1 = (s32[1,1024]{1,0:T(1,128)S(1)}, s32[1,1024]{1,0:T(1,128)S(1)}, u32[]{:S(2)}, u32[]{:S(2)}) collective-permute-start(s32[1,1024]{1,0:T(1,128)S(1)} %bitcast.4), channel_id=1, source_target_pairs={{4,0},{5,1},{6,2},{7,3},{8,4},{9,5},{10,6},{11,7},{12,8},{13,9},{1... | collective-permute-start | bytes 12296 | tf_op jit(solution)/shard_map/ppermute | solution.py:345
  22.9 3.1 %collective-permute-start = (s32[1,1024]{1,0:T(1,128)S(1)}, s32[1,1024]{1,0:T(1,128)S(1)}, u32[]{:S(2)}, u32[]{:S(2)}) collective-permute-start(s32[1,1024]{1,0:T(1,128)S(1)} %bitcast.5), channel_id=1, source_target_pairs={{2,0},{3,1},{4,2},{5,3},{6,4},{7,5},{8,6},{9,7},{10,8},{11,9},{12,... | collective-permute-start | bytes 12296 | tf_op jit(solution)/shard_map/ppermute | solution.py:345
  26.0 0.0 copy-done.1
  26.1 43.7 %collective-permute-done.1.refs_2_ = s32[1,1024]{1,0:T(1,128)S(1)} collective-permute-done((s32[1,1024]{1,0:T(1,128)S(1)}, s32[1,1024]{1,0:T(1,128)S(1)}, u32[]{:S(2)}, u32[]{:S(2)}) %collective-permute-start.1) | collective-permute-done | bytes 4128 | tf_op jit(solution)/shard_map/ppermute | solution.py:345
  69.8 0.0 collective-permute-done.refs_1_
  69.8 3.9 %all-to-all-done.got_hbm = bf16[64,296,128]{2,1,0:T(8,128)(2,1)} async-done(((bf16[64,296,128]{2,1,0:T(8,128)(2,1)}), bf16[64,296,128]{2,1,0:T(8,128)(2,1)}, u32[]{:S(2)}, u32[]{:S(2)}) %all-to-all-start) | async-done | bytes 4849696 | tf_op jit(solution)/shard_map/all_to_all | solution.py:363
  73.6 2.6 %shard_map.47 = (bf16[1040,768]{1,0:T(8,128)(2,1)S(1)}, bf16[3,64,16,768]{3,2,1,0:T(8,128)(2,1)S(1)}, f32[3,1,1024]{2,1,0:T(1,128)S(1)}, s32[1,1024]{1,0:T(1,128)S(1)}) custom-call(bf16[64,296,128]{2,1,0:T(8,128)(2,1)} %all-to-all-done.got_hbm, s32[1,128]{1,0:T(1,128)S(1)} %pad.4.list_ref, s32[1,1024]{1,0:T(1,128)S(1)} %bitcast.6, ...), custom_call_target="tpu_custom_call" | custom-call | flops 16106127360 | bytes 47185920 | tf_op jit(solution)/shard_map/pallas_call | solution.py:324
  76.3 2.0 %collective-permute-start.2 = (bf16[1040,768]{1,0:T(8,128)(2,1)S(1)}, bf16[1040,768]{1,0:T(8,128)(2,1)S(1)}, u32[]{:S(2)}, u32[]{:S(2)}) collective-permute-start(bf16[1040,768]{1,0:T(8,128)(2,1)S(1)} %get-tuple-element.14.own_ref), channel_id=1, source_target_pairs={{0,1},{1,0},{2,3},{3,2},{4,5},{5,4},{6,7},{7,6},{8,9},{9,8},{10,11... | collective-permute-start | bytes 4792328 | tf_op jit(solution)/shard_map/ppermute | solution.py:345
  78.2 2.8 %shard_map.48.sums_ref = f32[3,1,1024]{2,1,0:T(1,128)S(1)} custom-call(bf16[1040,768]{1,0:T(8,128)(2,1)S(1)} %get-tuple-element.14.own_ref, bf16[3,64,16,768]{3,2,1,0:T(8,128)(2,1)S(1)} %get-tuple-element.15.blocks_ref, f32[3,1,1024]{2,1,0:T(1,128)S(1)} %get-tuple-element.16.ids_ref), custom_call_target="tpu_custom_call" | custom-call | flops 64424509440 | bytes 94371840 | tf_op jit(solution)/shard_map/pallas_call | solution.py:324
  81.0 0.3 collective-permute-done.2.sw_ref
  81.3 2.5 %shard_map.49 = (f32[1,1024]{1,0:T(1,128)S(1)}, f32[1,1024]{1,0:T(1,128)S(1)}, f32[1,1024]{1,0:T(1,128)S(1)}, f32[1,1024]{1,0:T(1,128)S(1)}) custom-call(s32[1]{0:T(128)} %bitcast.2.core_ref, bf16[3,64,16,768]{3,2,1,0:T(8,128)(2,1)S(1)} %get-tuple-element.15.blocks_ref, f32[3,1,1024]{2,1,0:T(1,128)S(1)} %get-tuple-element.16.ids_ref, ...), custom_call_target="tpu_custom_call" | custom-call | flops 64424509440 | bytes 94371840 | tf_op jit(solution)/shard_map/pallas_call | solution.py:324
  83.9 0.5 collective-permute-start.3
  84.3 3.8 %collective-permute-start.4 = (f32[1,1024]{1,0:T(1,128)S(1)}, f32[1,1024]{1,0:T(1,128)S(1)}, u32[]{:S(2)}, u32[]{:S(2)}) collective-permute-start(f32[1,1024]{1,0:T(1,128)S(1)} %get-tuple-element.19), channel_id=1, source_target_pairs={{0,2},{1,3},{2,4},{3,5},{4,6},{5,7},{6,8},{7,9},{8,10},{9,11},{10,... | collective-permute-start | bytes 12296 | tf_op jit(solution)/shard_map/ppermute | solution.py:345
  88.1 2.8 %collective-permute-start.5 = (f32[1,1024]{1,0:T(1,128)S(1)}, f32[1,1024]{1,0:T(1,128)S(1)}, u32[]{:S(2)}, u32[]{:S(2)}) collective-permute-start(f32[1,1024]{1,0:T(1,128)S(1)} %get-tuple-element.20), channel_id=1, source_target_pairs={{0,4},{1,5},{2,6},{3,7},{4,8},{5,9},{6,10},{7,11},{8,12},{9,13},{1... | collective-permute-start | bytes 12296 | tf_op jit(solution)/shard_map/ppermute | solution.py:345
  90.9 1.4 %shard_map.50.refs_0_ = f32[1,1024]{1,0:T(1,128)S(1)} custom-call(bf16[1040,768]{1,0:T(8,128)(2,1)S(1)} %get-tuple-element.14.own_ref, f32[1,1024]{1,0:T(1,128)S(1)} %get-tuple-element.17.sum_ref), custom_call_target="tpu_custom_call" | custom-call | flops 19327352832 | bytes 50331648 | tf_op jit(solution)/shard_map/pallas_call | solution.py:324
  92.4 0.0 collective-permute-done.3.refs_1_
  92.4 1.9 %collective-permute-done.4.refs_2_ = f32[1,1024]{1,0:T(1,128)S(1)} collective-permute-done((f32[1,1024]{1,0:T(1,128)S(1)}, f32[1,1024]{1,0:T(1,128)S(1)}, u32[]{:S(2)}, u32[]{:S(2)}) %collective-permute-start.4) | collective-permute-done | bytes 4128 | tf_op jit(solution)/shard_map/ppermute | solution.py:345
  94.3 4.1 %collective-permute-done.5.refs_3_ = f32[1,1024]{1,0:T(1,128)S(1)} collective-permute-done((f32[1,1024]{1,0:T(1,128)S(1)}, f32[1,1024]{1,0:T(1,128)S(1)}, u32[]{:S(2)}, u32[]{:S(2)}) %collective-permute-start.5) | collective-permute-done | bytes 4128 | tf_op jit(solution)/shard_map/ppermute | solution.py:345
  98.4 1.3 %shard_map.51 = f32[1,1024]{1,0:T(1,128)} custom-call(s32[1,1024]{1,0:T(1,128)S(1)} %get-tuple-element.13.land_ref, f32[1,1024]{1,0:T(1,128)S(1)} %shard_map.50.refs_0_, f32[1,1024]{1,0:T(1,128)S(1)} %collective-permute-done.3.refs_1_, f32[1,1024]{1,0:T(1,128)S(1)} %collective-permute-done.4.refs_2_, f32[1,1024]{1,0:T(1,128)S(1)} %collective-permute-done.5.refs_3_), custom_call_target="tpu_custom_call" | custom-call | flops 6442450944 | bytes 37748736 | tf_op jit(solution)/shard_map/pallas_call | solution.py:324
  (2 shorter events, 0.0 us)
Async XLA Ops:
  5.3 10.4 %copy-start = (s32[1024]{0:T(1024)S(1)}, s32[1024]{0:T(1024)}, u32[]{:S(2)}) copy-start(s32[1024]{0:T(1024)} %param.6) | copy-start | bytes 12292
  5.3 20.8 %copy-start.1 = (s32[1,4]{1,0:T(1,128)S(1)}, s32[1,4]{1,0:T(1,128)}, u32[]{:S(2)}) copy-start(s32[1,4]{1,0:T(1,128)} %param.7) | copy-start | bytes 52
  5.3 68.3 %all-to-all-start = ((bf16[64,296,128]{2,1,0:T(8,128)(2,1)}), bf16[64,296,128]{2,1,0:T(8,128)(2,1)}, u32[]{:S(2)}, u32[]{:S(2)}) async-start(bf16[64,296,128]{2,1,0:T(8,128)(2,1)} %shard_map.46), calls=%async_computation | async-start | bytes 9699328 | tf_op jit(solution)/shard_map/all_to_all | solution.py:363
  15.6 54.1 %collective-permute-start.1 = (s32[1,1024]{1,0:T(1,128)S(1)}, s32[1,1024]{1,0:T(1,128)S(1)}, u32[]{:S(2)}, u32[]{:S(2)}) collective-permute-start(s32[1,1024]{1,0:T(1,128)S(1)} %bitcast.4), channel_id=1, source_target_pairs={{4,0},{5,1},{6,2},{7,3},{8,4},{9,5},{10,6},{11,7},{12,8},{13,9},{1... | collective-permute-start | bytes 12296 | tf_op jit(solution)/shard_map/ppermute | solution.py:345
  22.9 46.8 %collective-permute-start = (s32[1,1024]{1,0:T(1,128)S(1)}, s32[1,1024]{1,0:T(1,128)S(1)}, u32[]{:S(2)}, u32[]{:S(2)}) collective-permute-start(s32[1,1024]{1,0:T(1,128)S(1)} %bitcast.5), channel_id=1, source_target_pairs={{2,0},{3,1},{4,2},{5,3},{6,4},{7,5},{8,6},{9,7},{10,8},{11,9},{12,... | collective-permute-start | bytes 12296 | tf_op jit(solution)/shard_map/ppermute | solution.py:345
  76.3 5.1 %collective-permute-start.2 = (bf16[1040,768]{1,0:T(8,128)(2,1)S(1)}, bf16[1040,768]{1,0:T(8,128)(2,1)S(1)}, u32[]{:S(2)}, u32[]{:S(2)}) collective-permute-start(bf16[1040,768]{1,0:T(8,128)(2,1)S(1)} %get-tuple-element.14.own_ref), channel_id=1, source_target_pairs={{0,1},{1,0},{2,3},{3,2},{4,5},{5,4},{6,7},{7,6},{8,9},{9,8},{10,11... | collective-permute-start | bytes 4792328 | tf_op jit(solution)/shard_map/ppermute | solution.py:345
  83.9 8.5 %collective-permute-start.3 = (f32[1,1024]{1,0:T(1,128)S(1)}, f32[1,1024]{1,0:T(1,128)S(1)}, u32[]{:S(2)}, u32[]{:S(2)}) collective-permute-start(f32[1,1024]{1,0:T(1,128)S(1)} %get-tuple-element.18), channel_id=1, source_target_pairs={{0,1},{1,0},{2,3},{3,2},{4,5},{5,4},{6,7},{7,6},{8,9},{9,8},{10,11... | collective-permute-start | bytes 12296 | tf_op jit(solution)/shard_map/ppermute | solution.py:345
  84.3 10.0 %collective-permute-start.4 = (f32[1,1024]{1,0:T(1,128)S(1)}, f32[1,1024]{1,0:T(1,128)S(1)}, u32[]{:S(2)}, u32[]{:S(2)}) collective-permute-start(f32[1,1024]{1,0:T(1,128)S(1)} %get-tuple-element.19), channel_id=1, source_target_pairs={{0,2},{1,3},{2,4},{3,5},{4,6},{5,7},{6,8},{7,9},{8,10},{9,11},{10,... | collective-permute-start | bytes 12296 | tf_op jit(solution)/shard_map/ppermute | solution.py:345
  88.1 10.3 %collective-permute-start.5 = (f32[1,1024]{1,0:T(1,128)S(1)}, f32[1,1024]{1,0:T(1,128)S(1)}, u32[]{:S(2)}, u32[]{:S(2)}) collective-permute-start(f32[1,1024]{1,0:T(1,128)S(1)} %get-tuple-element.20), channel_id=1, source_target_pairs={{0,4},{1,5},{2,6},{3,7},{4,8},{5,9},{6,10},{7,11},{8,12},{9,13},{1... | collective-permute-start | bytes 12296 | tf_op jit(solution)/shard_map/ppermute | solution.py:345

commit v7 on v6

--- a/solution.py
+++ b/solution.py
@@ -39,8 +39,8 @@
 
 
 def one_hot(rows, first, wanted):
-    hit = iota((rows, wanted.shape[1]), 0) + first == wanted
-    return jnp.where(hit, 1.0, 0.0).astype(BF16)
+    hit = iota((rows, wanted.shape[1]), 0).astype(jnp.int16) == (wanted - first).astype(jnp.int16)
+    return jnp.where(hit, jnp.ones((), BF16), jnp.zeros((), BF16))
 
 
 def nt(a, b):

time: 102 us -> 103 us (level)
  starting transfers between devices: 29.8 us -> 31.1 us
    ppermute x6, starting transfers between devices: 19.4 us -> 20.7 us  [move(): return lax.ppermute(value, AXES, pairs)]
  transfers between devices with their start and end apart: 7 -> 7, of which waited for: 5 -> 4; matrix products, arithmetic and copies ran while one was open for 0% -> 0% of each run, Pallas kernels for 4% -> 6%
where the time goes in v7:
time: 103 us; the launch traced here: 101 us
  waiting for transfers between devices  54.5 us (53%)
  starting transfers between devices  31.1 us (30%)
  Pallas kernels  15.6 us (15%)
    ppermute x6, waiting for transfers between devices, move(): return lax.ppermute(value, AXES, pairs)  50.6 us
    ppermute x6, starting transfers between devices, move(): return lax.ppermute(value, AXES, pairs)  20.7 us
    pallas_call x6, Pallas kernels, call(): pl.pallas_call(kernel, out_shape=out_shape, in_specs=in_specs, out_specs=...  15.6 us
    all_to_all x1, starting transfers between devices, local(): lax.all_to_all(outgoing, AXES, split_axis=0, concat_axis=0, tiled=True)  10.4 us
    all_to_all x1, waiting for transfers between devices, local(): lax.all_to_all(outgoing, AXES, split_axis=0, concat_axis=0, tiled=True)  3.85 us
  transfers between devices with their start and end apart: 7, of which 4 were waited for; matrix products, arithmetic and copies ran while one was open for 0% of the time, Pallas kernels for 6%

profile of v7, /device:TPU:34, one launch (start us, length us, event | category | flops | bytes accessed | tf_op | source)
XLA Modules:
  0.0 101.3 jit_solution(13046167972310304991)
XLA Ops:
  0.0 5.2 %shard_map.46 = bf16[64,296,128]{2,1,0:T(8,128)(2,1)} custom-call(s32[1,1024]{1,0:T(1,128)} %bitcast.7, bf16[1024,768]{1,0:T(8,128)(2,1)} %emb_ref.1), custom_call_target="tpu_custom_call" | custom-call | flops 32212254720 | bytes 62914560 | tf_op jit(solution)/shard_map/pallas_call | solution.py:324
  5.2 0.0 copy-start
  5.2 0.0 copy-start.1
  5.3 10.4 %all-to-all-start = ((bf16[64,296,128]{2,1,0:T(8,128)(2,1)}), bf16[64,296,128]{2,1,0:T(8,128)(2,1)}, u32[]{:S(2)}, u32[]{:S(2)}) async-start(bf16[64,296,128]{2,1,0:T(8,128)(2,1)} %shard_map.46), calls=%async_computation | async-start | bytes 9699328 | tf_op jit(solution)/shard_map/all_to_all | solution.py:363
  15.6 0.0 copy-done
  15.6 7.3 %collective-permute-start.1 = (s32[1,1024]{1,0:T(1,128)S(1)}, s32[1,1024]{1,0:T(1,128)S(1)}, u32[]{:S(2)}, u32[]{:S(2)}) collective-permute-start(s32[1,1024]{1,0:T(1,128)S(1)} %bitcast.4), channel_id=1, source_target_pairs={{4,0},{5,1},{6,2},{7,3},{8,4},{9,5},{10,6},{11,7},{12,8},{13,9},{1... | collective-permute-start | bytes 12296 | tf_op jit(solution)/shard_map/ppermute | solution.py:345
  22.9 3.1 %collective-permute-start = (s32[1,1024]{1,0:T(1,128)S(1)}, s32[1,1024]{1,0:T(1,128)S(1)}, u32[]{:S(2)}, u32[]{:S(2)}) collective-permute-start(s32[1,1024]{1,0:T(1,128)S(1)} %bitcast.5), channel_id=1, source_target_pairs={{2,0},{3,1},{4,2},{5,3},{6,4},{7,5},{8,6},{9,7},{10,8},{11,9},{12,... | collective-permute-start | bytes 12296 | tf_op jit(solution)/shard_map/ppermute | solution.py:345
  26.0 0.0 copy-done.1
  26.1 43.7 %collective-permute-done.1.refs_2_ = s32[1,1024]{1,0:T(1,128)S(1)} collective-permute-done((s32[1,1024]{1,0:T(1,128)S(1)}, s32[1,1024]{1,0:T(1,128)S(1)}, u32[]{:S(2)}, u32[]{:S(2)}) %collective-permute-start.1) | collective-permute-done | bytes 4128 | tf_op jit(solution)/shard_map/ppermute | solution.py:345
  69.7 0.0 collective-permute-done.refs_1_
  69.7 3.9 %all-to-all-done.got_hbm = bf16[64,296,128]{2,1,0:T(8,128)(2,1)} async-done(((bf16[64,296,128]{2,1,0:T(8,128)(2,1)}), bf16[64,296,128]{2,1,0:T(8,128)(2,1)}, u32[]{:S(2)}, u32[]{:S(2)}) %all-to-all-start) | async-done | bytes 4849696 | tf_op jit(solution)/shard_map/all_to_all | solution.py:363
  73.6 2.6 %shard_map.47 = (bf16[1040,768]{1,0:T(8,128)(2,1)S(1)}, bf16[3,64,16,768]{3,2,1,0:T(8,128)(2,1)S(1)}, f32[3,1,1024]{2,1,0:T(1,128)S(1)}, s32[1,1024]{1,0:T(1,128)S(1)}) custom-call(bf16[64,296,128]{2,1,0:T(8,128)(2,1)} %all-to-all-done.got_hbm, s32[1,128]{1,0:T(1,128)S(1)} %pad.4.list_ref, s32[1,1024]{1,0:T(1,128)S(1)} %bitcast.6, ...), custom_call_target="tpu_custom_call" | custom-call | flops 16106127360 | bytes 47185920 | tf_op jit(solution)/shard_map/pallas_call | solution.py:324
  76.2 2.0 %collective-permute-start.2 = (bf16[1040,768]{1,0:T(8,128)(2,1)S(1)}, bf16[1040,768]{1,0:T(8,128)(2,1)S(1)}, u32[]{:S(2)}, u32[]{:S(2)}) collective-permute-start(bf16[1040,768]{1,0:T(8,128)(2,1)S(1)} %get-tuple-element.14.own_ref), channel_id=1, source_target_pairs={{0,1},{1,0},{2,3},{3,2},{4,5},{5,4},{6,7},{7,6},{8,9},{9,8},{10,11... | collective-permute-start | bytes 4792328 | tf_op jit(solution)/shard_map/ppermute | solution.py:345
  78.2 4.6 %shard_map.48.sums_ref = f32[3,1,1024]{2,1,0:T(1,128)S(1)} custom-call(bf16[1040,768]{1,0:T(8,128)(2,1)S(1)} %get-tuple-element.14.own_ref, bf16[3,64,16,768]{3,2,1,0:T(8,128)(2,1)S(1)} %get-tuple-element.15.blocks_ref, f32[3,1,1024]{2,1,0:T(1,128)S(1)} %get-tuple-element.16.ids_ref), custom_call_target="tpu_custom_call" | custom-call | flops 64424509440 | bytes 94371840 | tf_op jit(solution)/shard_map/pallas_call | solution.py:324
  82.8 0.0 collective-permute-done.2.sw_ref
  82.8 0.5 shard_map.49
  83.3 1.0 collective-permute-start.3
  84.3 5.5 %collective-permute-start.4 = (f32[1,1024]{1,0:T(1,128)S(1)}, f32[1,1024]{1,0:T(1,128)S(1)}, u32[]{:S(2)}, u32[]{:S(2)}) collective-permute-start(f32[1,1024]{1,0:T(1,128)S(1)} %get-tuple-element.19), channel_id=1, source_target_pairs={{0,2},{1,3},{2,4},{3,5},{4,6},{5,7},{6,8},{7,9},{8,10},{9,11},{10,... | collective-permute-start | bytes 12296 | tf_op jit(solution)/shard_map/ppermute | solution.py:345
  89.8 1.9 %collective-permute-start.5 = (f32[1,1024]{1,0:T(1,128)S(1)}, f32[1,1024]{1,0:T(1,128)S(1)}, u32[]{:S(2)}, u32[]{:S(2)}) collective-permute-start(f32[1,1024]{1,0:T(1,128)S(1)} %get-tuple-element.20), channel_id=1, source_target_pairs={{0,4},{1,5},{2,6},{3,7},{4,8},{5,9},{6,10},{7,11},{8,12},{9,13},{1... | collective-permute-start | bytes 12296 | tf_op jit(solution)/shard_map/ppermute | solution.py:345
  91.7 1.4 %shard_map.50.refs_0_ = f32[1,1024]{1,0:T(1,128)S(1)} custom-call(bf16[1040,768]{1,0:T(8,128)(2,1)S(1)} %get-tuple-element.14.own_ref, f32[1,1024]{1,0:T(1,128)S(1)} %get-tuple-element.17.sum_ref), custom_call_target="tpu_custom_call" | custom-call | flops 19327352832 | bytes 50331648 | tf_op jit(solution)/shard_map/pallas_call | solution.py:324
  93.1 0.0 collective-permute-done.3.refs_1_
  93.2 1.1 %collective-permute-done.4.refs_2_ = f32[1,1024]{1,0:T(1,128)S(1)} collective-permute-done((f32[1,1024]{1,0:T(1,128)S(1)}, f32[1,1024]{1,0:T(1,128)S(1)}, u32[]{:S(2)}, u32[]{:S(2)}) %collective-permute-start.4) | collective-permute-done | bytes 4128 | tf_op jit(solution)/shard_map/ppermute | solution.py:345
  94.3 5.8 %collective-permute-done.5.refs_3_ = f32[1,1024]{1,0:T(1,128)S(1)} collective-permute-done((f32[1,1024]{1,0:T(1,128)S(1)}, f32[1,1024]{1,0:T(1,128)S(1)}, u32[]{:S(2)}, u32[]{:S(2)}) %collective-permute-start.5) | collective-permute-done | bytes 4128 | tf_op jit(solution)/shard_map/ppermute | solution.py:345
  100.1 1.3 %shard_map.51 = f32[1,1024]{1,0:T(1,128)} custom-call(s32[1,1024]{1,0:T(1,128)S(1)} %get-tuple-element.13.land_ref, f32[1,1024]{1,0:T(1,128)S(1)} %shard_map.50.refs_0_, f32[1,1024]{1,0:T(1,128)S(1)} %collective-permute-done.3.refs_1_, f32[1,1024]{1,0:T(1,128)S(1)} %collective-permute-done.4.refs_2_, f32[1,1024]{1,0:T(1,128)S(1)} %collective-permute-done.5.refs_3_), custom_call_target="tpu_custom_call" | custom-call | flops 6442450944 | bytes 37748736 | tf_op jit(solution)/shard_map/pallas_call | solution.py:324
  (2 shorter events, 0.0 us)
Async XLA Ops:
  5.2 10.4 %copy-start = (s32[1024]{0:T(1024)S(1)}, s32[1024]{0:T(1024)}, u32[]{:S(2)}) copy-start(s32[1024]{0:T(1024)} %param.6) | copy-start | bytes 12292
  5.2 20.8 %copy-start.1 = (s32[1,4]{1,0:T(1,128)S(1)}, s32[1,4]{1,0:T(1,128)}, u32[]{:S(2)}) copy-start(s32[1,4]{1,0:T(1,128)} %param.7) | copy-start | bytes 52
  5.3 68.3 %all-to-all-start = ((bf16[64,296,128]{2,1,0:T(8,128)(2,1)}), bf16[64,296,128]{2,1,0:T(8,128)(2,1)}, u32[]{:S(2)}, u32[]{:S(2)}) async-start(bf16[64,296,128]{2,1,0:T(8,128)(2,1)} %shard_map.46), calls=%async_computation | async-start | bytes 9699328 | tf_op jit(solution)/shard_map/all_to_all | solution.py:363
  15.6 54.1 %collective-permute-start.1 = (s32[1,1024]{1,0:T(1,128)S(1)}, s32[1,1024]{1,0:T(1,128)S(1)}, u32[]{:S(2)}, u32[]{:S(2)}) collective-permute-start(s32[1,1024]{1,0:T(1,128)S(1)} %bitcast.4), channel_id=1, source_target_pairs={{4,0},{5,1},{6,2},{7,3},{8,4},{9,5},{10,6},{11,7},{12,8},{13,9},{1... | collective-permute-start | bytes 12296 | tf_op jit(solution)/shard_map/ppermute | solution.py:345
  22.9 46.8 %collective-permute-start = (s32[1,1024]{1,0:T(1,128)S(1)}, s32[1,1024]{1,0:T(1,128)S(1)}, u32[]{:S(2)}, u32[]{:S(2)}) collective-permute-start(s32[1,1024]{1,0:T(1,128)S(1)} %bitcast.5), channel_id=1, source_target_pairs={{2,0},{3,1},{4,2},{5,3},{6,4},{7,5},{8,6},{9,7},{10,8},{11,9},{12,... | collective-permute-start | bytes 12296 | tf_op jit(solution)/shard_map/ppermute | solution.py:345
  76.2 6.6 %collective-permute-start.2 = (bf16[1040,768]{1,0:T(8,128)(2,1)S(1)}, bf16[1040,768]{1,0:T(8,128)(2,1)S(1)}, u32[]{:S(2)}, u32[]{:S(2)}) collective-permute-start(bf16[1040,768]{1,0:T(8,128)(2,1)S(1)} %get-tuple-element.14.own_ref), channel_id=1, source_target_pairs={{0,1},{1,0},{2,3},{3,2},{4,5},{5,4},{6,7},{7,6},{8,9},{9,8},{10,11... | collective-permute-start | bytes 4792328 | tf_op jit(solution)/shard_map/ppermute | solution.py:345
  83.3 9.8 %collective-permute-start.3 = (f32[1,1024]{1,0:T(1,128)S(1)}, f32[1,1024]{1,0:T(1,128)S(1)}, u32[]{:S(2)}, u32[]{:S(2)}) collective-permute-start(f32[1,1024]{1,0:T(1,128)S(1)} %get-tuple-element.18), channel_id=1, source_target_pairs={{0,1},{1,0},{2,3},{3,2},{4,5},{5,4},{6,7},{7,6},{8,9},{9,8},{10,11... | collective-permute-start | bytes 12296 | tf_op jit(solution)/shard_map/ppermute | solution.py:345
  84.3 10.0 %collective-permute-start.4 = (f32[1,1024]{1,0:T(1,128)S(1)}, f32[1,1024]{1,0:T(1,128)S(1)}, u32[]{:S(2)}, u32[]{:S(2)}) collective-permute-start(f32[1,1024]{1,0:T(1,128)S(1)} %get-tuple-element.19), channel_id=1, source_target_pairs={{0,2},{1,3},{2,4},{3,5},{4,6},{5,7},{6,8},{7,9},{8,10},{9,11},{10,... | collective-permute-start | bytes 12296 | tf_op jit(solution)/shard_map/ppermute | solution.py:345
  89.8 10.3 %collective-permute-start.5 = (f32[1,1024]{1,0:T(1,128)S(1)}, f32[1,1024]{1,0:T(1,128)S(1)}, u32[]{:S(2)}, u32[]{:S(2)}) collective-permute-start(f32[1,1024]{1,0:T(1,128)S(1)} %get-tuple-element.20), channel_id=1, source_target_pairs={{0,4},{1,5},{2,6},{3,7},{4,8},{5,9},{6,10},{7,11},{8,12},{9,13},{1... | collective-permute-start | bytes 12296 | tf_op jit(solution)/shard_map/ppermute | solution.py:345
